TPU v7x, 256 devices: a whole 4x4x8 slice. The times are simulated.
256 devices in a mesh: dp: 8 (over y_lo, x), lon: 32 (over y_hi, z, core).
Axes of the slice: x: 4, y: 4 (y_hi: 2, y_lo: 2; y = y_hi * 2 + y_lo), z: 8, core: 2. Of those that a mesh axis runs over, the one named last changes fastest.
Arguments:
- fields: bfloat16 [8, 64, 512, 384], P('dp', None, 'lon'), may hold values from -6 to 6
- cotangent: bfloat16 [8, 64, 512, 384], P('dp', None, 'lon'), may hold values from -6 to 6
- kernel_first: bfloat16 [3, 3, 64, 64], replicated, may hold values from -0.25 to 0.25
- kernel_second: bfloat16 [3, 3, 64, 64], replicated, may hold values from -0.25 to 0.25
- metric: float32 [384], replicated, may hold values from 0.5 to 3
Outputs:
- field_grad: bfloat16 [8, 64, 512, 384], P('dp', None, 'lon')
- grad_first: bfloat16 [3, 3, 64, 64], replicated
- grad_second: bfloat16 [3, 3, 64, 64], replicated
All inputs are finite; a program needn't handle non-finite values.
Results may differ from a plain program's by a relative error of at most 0.0063.
Values may be sent and summed in bfloat16 or wider, within the bound.
A program may use at most 64 MiB of HBM per device.

v0:
```python
import jax
import jax.numpy as jnp
from jax import lax
from jax.sharding import PartitionSpec as P

gelu_coef = 0.7978845608


def extended(shard, sides, width):
    for axis, dim in sides:
        count, length = (lax.axis_size(axis), shard.shape[dim])
        up = [(i, (i + 1) % count) for i in range(count)]
        down = [(j, i) for i, j in up]
        last = lax.slice_in_dim(shard, length - width, length, axis=dim)
        first = lax.slice_in_dim(shard, 0, width, axis=dim)
        before = lax.ppermute(last, axis, up)
        after = lax.ppermute(first, axis, down)
        shard = jnp.concatenate([before, shard, after], axis=dim)
    return shard


def gelu_value(u):
    inner = jnp.tanh(gelu_coef * (u + 0.044715 * u * u * u))
    return 0.5 * u * (1.0 + inner)


def gelu_slope(u):
    inner = jnp.tanh(gelu_coef * (u + 0.044715 * u * u * u))
    return 0.5 * (1.0 + inner) + 0.5 * u * (1.0 - inner * inner) * gelu_coef * (
        1.0 + 3.0 * 0.044715 * u * u
    )


def pad_rows(value):
    return jnp.pad(value, ((0, 0), (0, 0), (0, 0), (1, 1)))


def stencil_apply(padded, taps, metric):
    columns = padded.shape[2] - 2
    lat_rows = padded.shape[3] - 2
    total = None
    for p in range(3):
        summed = None
        for q in range(3):
            term = jnp.einsum(
                "oc,bcij->boij",
                taps[p, q],
                padded[:, :, p : p + columns, q : q + lat_rows],
                preferred_element_type=jnp.float32,
            )
            summed = term if summed is None else summed + term
        summed = summed if p == 1 else summed * metric[None, None, None, :]
        total = summed if total is None else total + summed
    return total


def stencil_adjoint(plain_pad, scaled_pad, taps):
    columns = plain_pad.shape[2] - 2
    lat_rows = plain_pad.shape[3] - 2
    total = None
    for p in range(3):
        source = plain_pad if p == 1 else scaled_pad
        for q in range(3):
            term = jnp.einsum(
                "oc,boij->bcij",
                taps[p, q],
                source[:, :, 2 - p : 2 - p + columns, 2 - q : 2 - q + lat_rows],
                preferred_element_type=jnp.float32,
            )
            total = term if total is None else total + term
    return total


def kernel_term(plain, scaled, padded):
    columns = plain.shape[2]
    lat_rows = plain.shape[3]
    terms = []
    for p in range(3):
        source = plain if p == 1 else scaled
        row_terms = []
        for q in range(3):
            row_terms.append(
                jnp.einsum(
                    "boij,bcij->oc",
                    source,
                    padded[:, :, p : p + columns, q : q + lat_rows],
                    preferred_element_type=jnp.float32,
                )
            )
        terms.append(jnp.stack(row_terms))
    return jnp.stack(terms)


def per_device(fields, cotangent, kernel_first, kernel_second, metric):
    metric_padded = jnp.pad(metric, (1, 1))[None, None, None, :]
    samples_here = fields.shape[0]
    stacked = jnp.concatenate((fields, cotangent), axis=0)
    both_pad = extended(stacked, (("lon", 2),), 1)
    input_pad = pad_rows(both_pad[:samples_here])
    upstream_pad = pad_rows(both_pad[samples_here:])
    before_gelu = stencil_apply(input_pad, kernel_first, metric)
    hidden = gelu_value(before_gelu).astype(jnp.bfloat16)
    hidden_pad = pad_rows(extended(hidden, (("lon", 2),), 1))
    scaled_pad = (metric_padded * upstream_pad.astype(jnp.float32)).astype(jnp.bfloat16)
    second = kernel_term(cotangent, scaled_pad[:, :, 1:-1, 1:-1], hidden_pad)
    hidden_grad = stencil_adjoint(upstream_pad, scaled_pad, kernel_second)
    delta = (hidden_grad * gelu_slope(before_gelu)).astype(jnp.bfloat16)
    delta_pad = pad_rows(extended(delta, (("lon", 2),), 1))
    delta_scaled = (metric_padded * delta_pad.astype(jnp.float32)).astype(jnp.bfloat16)
    field_grad = (
        cotangent.astype(jnp.float32) + stencil_adjoint(delta_pad, delta_scaled, kernel_first)
    ).astype(jnp.bfloat16)
    first = kernel_term(delta, delta_scaled[:, :, 1:-1, 1:-1], input_pad)
    first, second = lax.psum((first, second), ("dp", "lon"))
    counted = (
        float(fields.shape[0] * lax.axis_size("dp"))
        * float(fields.shape[2] * lax.axis_size("lon"))
        * float(fields.shape[3])
    )
    factor = jnp.float32(1.0 / counted**0.5)
    return (
        field_grad,
        (first * factor).astype(jnp.bfloat16),
        (second * factor).astype(jnp.bfloat16),
    )


def solution(mesh):
    placed = (P("dp", None, "lon", None), P("dp", None, "lon", None), P(), P(), P())
    return jax.shard_map(
        per_device,
        mesh=mesh,
        in_specs=placed,
        out_specs=(P("dp", None, "lon", None), P(), P()),
        check_vma=False,
    )
```

profile of v0, /device:TPU:1, one launch (start us, length us, event | category | flops | bytes accessed | tf_op | source)
XLA Modules:
  0.0 325.4 jit_solution(10439744815576890022)
XLA Ops:
  7.2 1.4 copy_dynamic-update-slice_fusion
  9.0 3.1 collective-permute-start
  13.7 2.4 collective-permute-done.1
  16.6 0.4 fusion.53
  17.0 0.4 fusion.56
  17.5 0.4 fusion.59
  17.9 0.4 fusion.62
  18.3 0.4 fusion.65
  18.8 0.4 fusion.68
  19.6 1.2 multiply_convert_fusion.2
  21.1 0.6 multiply_convert_fusion.1
  21.7 0.4 fusion.38
  22.2 0.4 fusion.39
  23.0 0.4 fusion.41
  23.5 0.4 fusion.42
  24.4 0.4 fusion.15
  24.8 1.6 fusion.7
  28.1 4.7 %collective-permute-start.5 = (bf16[1,64,1,384]{3,1,2,0:T(8,128)(2,1)S(1)}, bf16[1,64,1,384]{3,1,2,0:T(8,128)(2,1)S(1)}, u32[]{:S(2)}, u32[]{:S(2)}) collective-permute-start(bf16[1,64,1,384]{3,1,2,0:T(8,128)(2,1)S(1)} %get-tuple-element.15), channel_id=1, source_target_pairs={{1,0},{2,1},{3,2},{4,3},{5,4},{6,5},{7,6},{8,7},{9,8},{10,9},{11,1... | collective-permute-start | bytes 147464 | tf_op jit(solution)/shard_map/ppermute | solution.py:17
  32.9 5.4 %collective-permute-start.3 = (bf16[1,64,1,384]{3,1,2,0:T(8,128)(2,1)S(1)}, bf16[1,64,1,384]{3,1,2,0:T(8,128)(2,1)S(1)}, u32[]{:S(2)}, u32[]{:S(2)}) collective-permute-start(bf16[1,64,1,384]{3,1,2,0:T(8,128)(2,1)S(1)} %get-tuple-element.17), channel_id=1, source_target_pairs={{1,0},{2,1},{3,2},{4,3},{5,4},{6,5},{7,6},{8,7},{9,8},{10,9},{11,1... | collective-permute-start | bytes 147464 | tf_op jit(solution)/shard_map/ppermute | solution.py:17
  38.3 0.7 select_maximum_fusion
  39.0 0.5 convolution_bitcast_fusion.3
  39.9 0.4 convolution_bitcast_fusion.2
  40.3 0.7 convolution_bitcast_fusion
  41.0 0.4 convolution_bitcast_fusion.8
  41.5 0.7 convolution_bitcast_fusion.6
  42.2 0.9 multiply_convert_fusion
  43.1 0.7 convolution_bitcast_fusion.11
  43.8 0.7 convolution_bitcast_fusion.15
  44.5 0.7 convolution_bitcast_fusion.17
  45.2 0.7 convolution_bitcast_fusion.9
  45.9 1.6 fusion.29
  47.5 1.6 fusion.30
  49.1 1.6 fusion.31
  50.7 1.7 fusion.32
  52.4 1.6 fusion.33
  53.9 1.6 fusion.34
  55.5 1.7 fusion.35
  57.3 0.5 convolution_bitcast_fusion.1
  57.8 0.5 convolution_bitcast_fusion.7
  58.3 0.8 pad_maximum_fusion.6
  59.0 0.5 convolution_bitcast_fusion.10
  59.5 0.5 convolution_bitcast_fusion.16
  60.0 0.7 pad_maximum_fusion.5
  60.8 5.4 %fusion.8 = bf16[1,64,16,384]{3,1,2,0:T(8,128)(2,1)S(1)} fusion(f32[16,384,64]{1,2,0:T(8,128)} %fusion.29, f32[16,384,64]{1,2,0:T(8,128)} %fusion.30, f32[16,384,64]{1,2,0:T(8,128)} %fusion.31, f32[16,384,64]{1,2,0:T(8,128)S(1)} %fusion.47, f32[16,384,64]{1,2,0:T(8,128)} %fusion.32, f32[16,384,64]{1,2,0:T(8,128)} %fusion.33, f32[16,384,64]{1,2,0:T(8,128)} %fusion.35, ...), kind=kOutput, calls=%fused_computation.16 | convolution fusion | flops 54657024 | bytes 14958592 | tf_op jit(solution)/shard_map/oc,boij->bcij/dot_general | solution.py:64
  66.2 1.3 copy.38
  67.5 247.8 %all-reduce.8.cloned.1.call-done = (f32[3,3,64,64]{3,2,1,0:T(8,128)}, f32[3,3,64,64]{3,2,1,0:T(8,128)}) async-done(((f32[3,3,64,64]{3,2,1,0:T(8,128)}, f32[3,3,64,64]{3,2,1,0:T(8,128)}), (f32[3,3,64,64]{3,2,1,0:T(8,128)}, f32[3,3,64,64]{3,2,1,0:T(8,128)})) %all-reduce.8.cloned.1.call-update) | async-done | bytes 294928 | tf_op jit(solution)/shard_map/psum | solution.py:114
  315.2 1.7 multiply_convert_fusion.3
  316.9 1.7 multiply_convert_fusion.4
  (44 shorter events, 6.1 us)
Async XLA Ops:
  7.2 5.2 %copy-start.1 = (bf16[1,64,16,384]{3,2,1,0:T(8,128)(2,1)S(1)}, bf16[1,64,16,384]{3,2,1,0:T(8,128)(2,1)}, u32[]{:S(2)}) copy-start(bf16[1,64,16,384]{3,2,1,0:T(8,128)(2,1)} %param.5) | copy-start | bytes 2359300
  7.2 1.5 copy-start
  7.2 5.2 %copy-start.2 = (bf16[3,3,64,64]{3,2,1,0:T(8,128)(2,1)S(1)}, bf16[3,3,64,64]{3,2,1,0:T(8,128)(2,1)}, u32[]{:S(2)}) copy-start(bf16[3,3,64,64]{3,2,1,0:T(8,128)(2,1)} %param.7) | copy-start | bytes 221188
  7.2 308.1 %all-reduce.8.cloned.1.call-start = ((), (), s32[]{:S(2)}) async-start(), calls=%async_computation | async-start | bytes 1179648 | tf_op jit(solution)/shard_map/psum | solution.py:114
  8.9 3.8 %copy-start.4 = (bf16[3,3,64,64]{3,2,1,0:T(8,128)(2,1)S(1)}, bf16[3,3,64,64]{3,2,1,0:T(8,128)(2,1)}, u32[]{:S(2)}) copy-start(bf16[3,3,64,64]{3,2,1,0:T(8,128)(2,1)} %param.8) | copy-start | bytes 221188
  9.0 4.7 %collective-permute-start = (bf16[2,64,1,384]{3,1,2,0:T(8,128)(2,1)S(1)}, bf16[2,64,1,384]{3,1,2,0:T(8,128)(2,1)S(1)}, u32[]{:S(2)}, u32[]{:S(2)}) collective-permute-start(bf16[2,64,1,384]{3,1,2,0:T(8,128)(2,1)S(1)} %get-tuple-element.12), channel_id=1, source_target_pairs={{0,1},{1,2},{2,3},{3,4},{4,5},{5,6},{6,7},{7,8},{8,9},{9,10},{10,1... | collective-permute-start | bytes 294920 | tf_op jit(solution)/shard_map/ppermute | solution.py:16
  12.1 4.0 %collective-permute-start.1 = (bf16[2,64,1,384]{3,1,2,0:T(8,128)(2,1)S(1)}, bf16[2,64,1,384]{3,1,2,0:T(8,128)(2,1)S(1)}, u32[]{:S(2)}, u32[]{:S(2)}) collective-permute-start(bf16[2,64,1,384]{3,1,2,0:T(8,128)(2,1)S(1)} %get-tuple-element.13), channel_id=1, source_target_pairs={{1,0},{2,1},{3,2},{4,3},{5,4},{6,5},{7,6},{8,7},{9,8},{10,9},{11,1... | collective-permute-start | bytes 294920 | tf_op jit(solution)/shard_map/ppermute | solution.py:17
  12.7 0.7 copy-start.5
  28.0 10.3 %collective-permute-start.4 = (bf16[1,64,1,384]{3,1,2,0:T(8,128)(2,1)S(1)}, bf16[1,64,1,384]{3,1,2,0:T(8,128)(2,1)S(1)}, u32[]{:S(2)}, u32[]{:S(2)}) collective-permute-start(bf16[1,64,1,384]{3,1,2,0:T(8,128)(2,1)S(1)} %get-tuple-element.14), channel_id=1, source_target_pairs={{0,1},{1,2},{2,3},{3,4},{4,5},{5,6},{6,7},{7,8},{8,9},{9,10},{10,1... | collective-permute-start | bytes 147464 | tf_op jit(solution)/shard_map/ppermute | solution.py:16
  28.1 10.2 %collective-permute-start.5 = (bf16[1,64,1,384]{3,1,2,0:T(8,128)(2,1)S(1)}, bf16[1,64,1,384]{3,1,2,0:T(8,128)(2,1)S(1)}, u32[]{:S(2)}, u32[]{:S(2)}) collective-permute-start(bf16[1,64,1,384]{3,1,2,0:T(8,128)(2,1)S(1)} %get-tuple-element.15), channel_id=1, source_target_pairs={{1,0},{2,1},{3,2},{4,3},{5,4},{6,5},{7,6},{8,7},{9,8},{10,9},{11,1... | collective-permute-start | bytes 147464 | tf_op jit(solution)/shard_map/ppermute | solution.py:17
  32.9 9.3 %collective-permute-start.2 = (bf16[1,64,1,384]{3,1,2,0:T(8,128)(2,1)S(1)}, bf16[1,64,1,384]{3,1,2,0:T(8,128)(2,1)S(1)}, u32[]{:S(2)}, u32[]{:S(2)}) collective-permute-start(bf16[1,64,1,384]{3,1,2,0:T(8,128)(2,1)S(1)} %get-tuple-element.16), channel_id=1, source_target_pairs={{0,1},{1,2},{2,3},{3,4},{4,5},{5,6},{6,7},{7,8},{8,9},{9,10},{10,1... | collective-permute-start | bytes 147464 | tf_op jit(solution)/shard_map/ppermute | solution.py:16
  32.9 9.3 %collective-permute-start.3 = (bf16[1,64,1,384]{3,1,2,0:T(8,128)(2,1)S(1)}, bf16[1,64,1,384]{3,1,2,0:T(8,128)(2,1)S(1)}, u32[]{:S(2)}, u32[]{:S(2)}) collective-permute-start(bf16[1,64,1,384]{3,1,2,0:T(8,128)(2,1)S(1)} %get-tuple-element.17), channel_id=1, source_target_pairs={{1,0},{2,1},{3,2},{4,3},{5,4},{6,5},{7,6},{8,7},{9,8},{10,9},{11,1... | collective-permute-start | bytes 147464 | tf_op jit(solution)/shard_map/ppermute | solution.py:17
  44.5 1.4 copy-start.3
Sparse Core Ops, SparseCore 0:
  60.9 254.3 all-reduce.7
where the time goes:
time: 326 us; the launch traced here: 325 us
  waiting for transfers between devices  250 us (77%)
  matrix products  36 us (11%)
  between operations  14.5 us (4%)
  starting transfers between devices  13.7 us (4%)
  other arithmetic  7.25 us (2%)
  local copies, waits for them, and re-layouts  3.62 us (1%)
    psum x1, waiting for transfers between devices, per_device(): first, second = lax.psum((first, second), ('dp', 'lon'))  248 us
    dot_general x18, matrix products, stencil_adjoint(): jnp.einsum('oc,boij->bcij', taps[p, q], source[:, :, 2 - p:2 - p + column...  22.2 us
    ppermute x3, starting transfers between devices, extended(): after = lax.ppermute(first, axis, down)  10.4 us
    dot_general x18, matrix products, kernel_term(): jnp.einsum('boij,bcij->oc', source, padded[:, :, p:p + columns, q:q + lat...  9.32 us
  transfers between devices with their start and end apart: 7, of which 3 were waited for; matrix products, arithmetic and copies ran while one was open for 3% of the time, Pallas kernels for 0%

commit v1 on v0

--- a/solution.py
+++ b/solution.py
@@ -1,7 +1,152 @@
+import functools
 import jax
 import jax.numpy as jnp
 from jax import lax
+from jax.experimental import pallas as pl
+from jax.experimental.pallas import tpu as pltpu
 from jax.sharding import PartitionSpec as P
+
+PLANE = 32
+DEEP = 8
+ROWS = 18
+MESH = pl.DeviceIdType.MESH
+
+
+def place():
+    dp = lax.axis_index("dp")
+    lon = lax.axis_index("lon")
+    core = lon % 2
+    z = (lon // 2) % DEEP
+    high = lon // (2 * DEEP)
+    return dp, lon, z, dp * 4 + high * 2 + core
+
+
+def plane_device(member, z):
+    return (member // 4, ((member // 2) % 2) * (2 * DEEP) + z * 2 + member % 2)
+
+
+def greet():
+    dp, lon, z, member = place()
+    barrier = pltpu.get_barrier_semaphore()
+
+    def to_plane(k, carry):
+        peer = (member + k) % PLANE
+        pl.semaphore_signal(barrier, inc=1, device_id=plane_device(peer, z), device_id_type=MESH)
+        return carry
+
+    def to_deep(k, carry):
+        peer = (z + k) % DEEP
+        pl.semaphore_signal(barrier, inc=1, device_id=plane_device(member, peer), device_id_type=MESH)
+        return carry
+
+    lax.fori_loop(1, PLANE, to_plane, 0)
+    lax.fori_loop(1, DEEP, to_deep, 0)
+    return barrier
+
+
+def all_reduce(x_ref, factor, out, parts, zparts, whole, plane_send, plane_recv, deep_send, deep_recv, gather_send, gather_recv):
+    dp, lon, z, member = place()
+    for g in range(PLANE):
+        out[g] = x_ref[g * ROWS:(g + 1) * ROWS, :].astype(out.dtype)
+
+    def scatter(k):
+        peer = (member + k) % PLANE
+        back = (member + PLANE - k) % PLANE
+        return pltpu.make_async_remote_copy(
+            src_ref=out.at[peer], dst_ref=parts.at[member], send_sem=plane_send.at[peer], recv_sem=plane_recv.at[member],
+            device_id=plane_device(peer, z), device_id_type=MESH)
+
+    def arrive(k):
+        peer = (member + k) % PLANE
+        return pltpu.make_async_remote_copy(
+            src_ref=out.at[peer], dst_ref=parts.at[peer], send_sem=plane_send.at[peer], recv_sem=plane_recv.at[peer],
+            device_id=plane_device(peer, z), device_id_type=MESH)
+
+    def run(start, stop, fn):
+        def step(k, carry):
+            fn(k)
+            return carry
+        lax.fori_loop(start, stop, step, 0)
+
+    run(1, PLANE, lambda k: scatter(k).start())
+    parts[member] = out[member]
+    run(1, PLANE, lambda k: arrive(k).wait_recv())
+    total = parts[0].astype(jnp.float32)
+    for g in range(1, PLANE):
+        total = total + parts[g].astype(jnp.float32)
+    zparts[z] = total.astype(zparts.dtype)
+
+    def deep(k):
+        peer = (z + k) % DEEP
+        return pltpu.make_async_remote_copy(
+            src_ref=zparts.at[z], dst_ref=zparts.at[z], send_sem=deep_send.at[peer], recv_sem=deep_recv.at[z],
+            device_id=plane_device(member, peer), device_id_type=MESH)
+
+    def deep_in(k):
+        peer = (z + k) % DEEP
+        return pltpu.make_async_remote_copy(
+            src_ref=zparts.at[z], dst_ref=zparts.at[peer], send_sem=deep_send.at[peer], recv_sem=deep_recv.at[peer],
+            device_id=plane_device(member, peer), device_id_type=MESH)
+
+    run(1, DEEP, lambda k: deep(k).start())
+    run(1, DEEP, lambda k: deep_in(k).wait_recv())
+    total = zparts[0].astype(jnp.float32)
+    for g in range(1, DEEP):
+        total = total + zparts[g].astype(jnp.float32)
+    whole[member] = (total * factor).astype(whole.dtype)
+
+    def gather(k):
+        peer = (member + k) % PLANE
+        return pltpu.make_async_remote_copy(
+            src_ref=whole.at[member], dst_ref=whole.at[member], send_sem=gather_send.at[peer], recv_sem=gather_recv.at[member],
+            device_id=plane_device(peer, z), device_id_type=MESH)
+
+    def gathered(k):
+        peer = (member + k) % PLANE
+        return pltpu.make_async_remote_copy(
+            src_ref=whole.at[member], dst_ref=whole.at[peer], send_sem=gather_send.at[peer], recv_sem=gather_recv.at[peer],
+            device_id=plane_device(peer, z), device_id_type=MESH)
+
+    run(1, PLANE, lambda k: gather(k).start())
+    run(1, PLANE, lambda k: gathered(k).wait_recv())
+    run(1, PLANE, lambda k: scatter(k).wait_send())
+    run(1, DEEP, lambda k: deep(k).wait_send())
+    run(1, PLANE, lambda k: gather(k).wait_send())
+
+
+def reduce_kernel(factor, x_ref, y_ref, *scratch):
+    barrier = greet()
+    pl.semaphore_wait(barrier, PLANE + DEEP - 2)
+    all_reduce(x_ref, factor, *scratch)
+    whole = scratch[3]
+    for g in range(PLANE):
+        y_ref[g * ROWS:(g + 1) * ROWS, :] = whole[g].astype(jnp.float32)
+
+
+def reduce_scratch():
+    return [
+        pltpu.VMEM((PLANE, ROWS, 128), jnp.bfloat16),
+        pltpu.VMEM((PLANE, ROWS, 128), jnp.bfloat16),
+        pltpu.VMEM((DEEP, ROWS, 128), jnp.float32),
+        pltpu.VMEM((PLANE, ROWS, 128), jnp.bfloat16),
+        pltpu.SemaphoreType.DMA((PLANE,)),
+        pltpu.SemaphoreType.DMA((PLANE,)),
+        pltpu.SemaphoreType.DMA((DEEP,)),
+        pltpu.SemaphoreType.DMA((DEEP,)),
+        pltpu.SemaphoreType.DMA((PLANE,)),
+        pltpu.SemaphoreType.DMA((PLANE,)),
+    ]
+
+
+def reduced(grads, factor):
+    return pl.pallas_call(
+        functools.partial(reduce_kernel, factor),
+        out_shape=jax.ShapeDtypeStruct((PLANE * ROWS, 128), jnp.float32),
+        in_specs=[pl.BlockSpec(memory_space=pltpu.VMEM)],
+        out_specs=pl.BlockSpec(memory_space=pltpu.VMEM),
+        scratch_shapes=reduce_scratch(),
+        compiler_params=pltpu.CompilerParams(collective_id=0, has_side_effects=True),
+    )(grads)
 
 gelu_coef = 0.7978845608
 
@@ -111,18 +256,15 @@
         cotangent.astype(jnp.float32) + stencil_adjoint(delta_pad, delta_scaled, kernel_first)
     ).astype(jnp.bfloat16)
     first = kernel_term(delta, delta_scaled[:, :, 1:-1, 1:-1], input_pad)
-    first, second = lax.psum((first, second), ("dp", "lon"))
     counted = (
         float(fields.shape[0] * lax.axis_size("dp"))
         * float(fields.shape[2] * lax.axis_size("lon"))
         * float(fields.shape[3])
     )
-    factor = jnp.float32(1.0 / counted**0.5)
-    return (
-        field_grad,
-        (first * factor).astype(jnp.bfloat16),
-        (second * factor).astype(jnp.bfloat16),
-    )
+    both = jnp.stack((first, second))
+    done = reduced(both.reshape(PLANE * ROWS, 128), 1.0 / counted**0.5)
+    done = done.reshape(both.shape).astype(jnp.bfloat16)
+    return field_grad, done[0], done[1]
 
 
 def solution(mesh):

time: 326 us -> 97.1 us (0.30)
  waiting for transfers between devices: 250 us -> 2.64 us
  Pallas kernels: 0 us -> 29.4 us
  between operations: 14.5 us -> 1.1 us
  local copies, waits for them, and re-layouts: 3.62 us -> 9.53 us
    psum x1 -> x0, waiting for transfers between devices: 248 us -> none  [per_device(): first, second = lax.psum((first, second), ('dp', 'lon'))]
    pallas_call x0 -> x1, Pallas kernels: none -> 29.4 us  [reduced(): pl.pallas_call(functools.partial(reduce_kernel, factor), out_shape=jax.Sh...]
    squeeze x0 -> x2, local copies, waits for them, and re-layouts: none -> 3.31 us  [per_device(): return (field_grad, done[0], done[1])]
  transfers between devices with their start and end apart: 7 -> 6, of which waited for: 3 -> 2; matrix products, arithmetic and copies ran while one was open for 3% -> 5% of each run, Pallas kernels for 0% -> 0%
where the time goes in v1:
time: 97.1 us; the launch traced here: 96.8 us
  matrix products  35.9 us (37%)
  Pallas kernels  29.4 us (30%)
  starting transfers between devices  13.8 us (14%)
  local copies, waits for them, and re-layouts  9.53 us (10%)
  other arithmetic  4.36 us (4%)
  waiting for transfers between devices  2.64 us (3%)
  between operations  1.1 us (1%)
    pallas_call x1, Pallas kernels, reduced(): pl.pallas_call(functools.partial(reduce_kernel, factor), out_shape=jax.Sh...  29.4 us
    dot_general x18, matrix products, stencil_adjoint(): jnp.einsum('oc,boij->bcij', taps[p, q], source[:, :, 2 - p:2 - p + column...  22.2 us
    ppermute x3, starting transfers between devices, extended(): after = lax.ppermute(first, axis, down)  10.5 us
    dot_general x18, matrix products, kernel_term(): jnp.einsum('boij,bcij->oc', source, padded[:, :, p:p + columns, q:q + lat...  9.26 us
    dot_general x9, matrix products, stencil_apply(): jnp.einsum('oc,bcij->boij', taps[p, q], padded[:, :, p:p + columns, q:q +...  4.49 us
    ppermute x3, starting transfers between devices, extended(): before = lax.ppermute(last, axis, up)  3.36 us
    squeeze x2, local copies, waits for them, and re-layouts, per_device(): return (field_grad, done[0], done[1])  3.31 us
    unnamed x12, local copies, waits for them, and re-layouts  3.07 us
  transfers between devices with their start and end apart: 6, of which 2 were waited for; matrix products, arithmetic and copies ran while one was open for 5% of the time, Pallas kernels for 0%

profile of v1, /device:TPU:1, one launch (start us, length us, event | category | flops | bytes accessed | tf_op | source)
XLA Modules:
  0.0 96.8 jit_solution(5024019208318006621)
XLA Ops:
  0.7 1.4 %copy_dynamic-update-slice_fusion = bf16[2,64,16,384]{3,1,2,0:T(8,128)(2,1)S(1)} fusion(bf16[1,64,16,384]{3,2,1,0:T(8,128)(2,1)} %param.5), kind=kLoop, calls=%fused_computation.114 | loop fusion | bytes 1572864
  2.4 3.1 %collective-permute-start = (bf16[2,64,1,384]{3,1,2,0:T(8,128)(2,1)S(1)}, bf16[2,64,1,384]{3,1,2,0:T(8,128)(2,1)S(1)}, u32[]{:S(2)}, u32[]{:S(2)}) collective-permute-start(bf16[2,64,1,384]{3,1,2,0:T(8,128)(2,1)S(1)} %get-tuple-element.10), channel_id=1, source_target_pairs={{0,1},{1,2},{2,3},{3,4},{4,5},{5,6},{6,7},{7,8},{8,9},{9,10},{10,1... | collective-permute-start | bytes 294920 | tf_op jit(solution)/shard_map/ppermute | solution.py:161
  7.2 2.4 %collective-permute-done.1 = bf16[2,64,1,384]{3,1,2,0:T(8,128)(2,1)S(1)} collective-permute-done((bf16[2,64,1,384]{3,1,2,0:T(8,128)(2,1)S(1)}, bf16[2,64,1,384]{3,1,2,0:T(8,128)(2,1)S(1)}, u32[]{:S(2)}, u32[]{:S(2)}) %collective-permute-start.1) | collective-permute-done | bytes 98336 | tf_op jit(solution)/shard_map/ppermute | solution.py:162
  10.0 0.4 fusion.53
  10.5 0.4 fusion.56
  10.9 0.4 fusion.59
  11.3 0.4 fusion.62
  11.8 0.4 fusion.65
  12.2 0.4 fusion.68
  12.7 0.6 multiply_convert_fusion.1
  13.3 0.4 fusion.38
  13.7 0.4 fusion.39
  14.5 0.4 fusion.41
  15.0 0.4 fusion.42
  15.4 0.4 fusion.12
  16.7 1.2 %multiply_convert_fusion.2 = (bf16[1,64,16,384]{3,1,2,0:T(8,128)(2,1)S(1)}, f32[1,16,384,64]{2,3,1,0:T(8,128)S(1)}) fusion(f32[16,384,64]{1,2,0:T(8,128)S(1)} %fusion.53, f32[16,384,64]{1,2,0:T(8,128)S(1)} %fusion.56, bf16[2,64,1,384]{3,1,2,0:T(8,128)(2,1)S(1)} %collective-permute-done.1, bf16[2,64,16,384]{3,1,2,0:T(8,128)(2,1)S(1)} %copy_dynamic-update-slice_fusion.1, ...), kind=kOutput, calls=%fused_computation.22 | convolution fusion | flops 59375616 | bytes 16631808 | tf_op jit(solution)/shard_map/oc,bcij->boij/dot_general | solution.py:190
  17.8 1.5 %fusion.7 = bf16[1,64,16,384]{3,1,2,0:T(8,128)(2,1)S(1)} fusion(f32[1,16,384,64]{2,3,1,0:T(8,128)S(1)} %get-tuple-element.19, f32[16,384,64]{1,2,0:T(8,128)S(1)} %fusion.38, f32[16,384,64]{1,2,0:T(8,128)S(1)} %fusion.39, f32[16,384,64]{1,2,0:T(8,128)S(1)} %fusion.15, f32[16,384,64]{1,2,0:T(8,128)S(1)} %fusion.73, f32[16,384,64]{1,2,0:T(8,128)S(1)} %fusion.12, ...), kind=kOutput, calls=%fused_computation.14 | convolution fusion | flops 60948480 | bytes 15745024 | tf_op jit(solution)/shard_map/oc,boij->bcij/dot_general | solution.py:209
  21.7 4.8 %collective-permute-start.3 = (bf16[1,64,1,384]{3,1,2,0:T(8,128)(2,1)S(1)}, bf16[1,64,1,384]{3,1,2,0:T(8,128)(2,1)S(1)}, u32[]{:S(2)}, u32[]{:S(2)}) collective-permute-start(bf16[1,64,1,384]{3,1,2,0:T(8,128)(2,1)S(1)} %get-tuple-element.15), channel_id=1, source_target_pairs={{1,0},{2,1},{3,2},{4,3},{5,4},{6,5},{7,6},{8,7},{9,8},{10,9},{11,1... | collective-permute-start | bytes 147464 | tf_op jit(solution)/shard_map/ppermute | solution.py:162
  26.5 5.4 %collective-permute-start.5 = (bf16[1,64,1,384]{3,1,2,0:T(8,128)(2,1)S(1)}, bf16[1,64,1,384]{3,1,2,0:T(8,128)(2,1)S(1)}, u32[]{:S(2)}, u32[]{:S(2)}) collective-permute-start(bf16[1,64,1,384]{3,1,2,0:T(8,128)(2,1)S(1)} %get-tuple-element.13), channel_id=1, source_target_pairs={{1,0},{2,1},{3,2},{4,3},{5,4},{6,5},{7,6},{8,7},{9,8},{10,9},{11,1... | collective-permute-start | bytes 147464 | tf_op jit(solution)/shard_map/ppermute | solution.py:162
  31.9 0.9 multiply_convert_fusion
  32.8 0.7 convolution_bitcast_fusion.11
  33.5 0.7 convolution_bitcast_fusion.15
  34.2 0.7 convolution_bitcast_fusion.17
  34.9 0.7 convolution_bitcast_fusion.9
  35.6 0.7 select_maximum_fusion
  36.3 0.5 convolution_bitcast_fusion.3
  37.6 0.7 convolution_bitcast_fusion
  38.7 0.7 convolution_bitcast_fusion.6
  39.4 1.7 %fusion.29 = f32[16,384,64]{1,2,0:T(8,128)} fusion(bf16[1,64,18,386]{3,1,2,0:T(8,128)(2,1)S(1)} %get-tuple-element.6, bf16[3,3,64,64]{3,2,1,0:T(8,128)(2,1)S(1)} %copy-done.2), kind=kOutput, calls=%fused_computation.80 | convolution fusion | flops 50331648 | bytes 2375680 | tf_op jit(solution)/shard_map/oc,boij->bcij/dot_general | solution.py:209
  41.1 1.6 %fusion.30 = f32[16,384,64]{1,2,0:T(8,128)} fusion(bf16[1,64,18,386]{3,1,2,0:T(8,128)(2,1)S(1)} %get-tuple-element.6, bf16[3,3,64,64]{3,2,1,0:T(8,128)(2,1)S(1)} %copy-done.2), kind=kOutput, calls=%fused_computation.82 | convolution fusion | flops 50331648 | bytes 2375680 | tf_op jit(solution)/shard_map/oc,boij->bcij/dot_general | solution.py:209
  42.7 1.6 %fusion.31 = f32[16,384,64]{1,2,0:T(8,128)} fusion(bf16[1,64,18,386]{3,1,2,0:T(8,128)(2,1)S(1)} %get-tuple-element.7, bf16[3,3,64,64]{3,2,1,0:T(8,128)(2,1)S(1)} %copy-done.2), kind=kOutput, calls=%fused_computation.84 | convolution fusion | flops 50331648 | bytes 2375680 | tf_op jit(solution)/shard_map/oc,boij->bcij/dot_general | solution.py:209
  44.3 1.7 %fusion.32 = f32[16,384,64]{1,2,0:T(8,128)} fusion(bf16[1,64,18,386]{3,1,2,0:T(8,128)(2,1)S(1)} %get-tuple-element.7, bf16[3,3,64,64]{3,2,1,0:T(8,128)(2,1)S(1)} %copy-done.2), kind=kOutput, calls=%fused_computation.86 | convolution fusion | flops 50331648 | bytes 2375680 | tf_op jit(solution)/shard_map/oc,boij->bcij/dot_general | solution.py:209
  45.9 1.6 %fusion.33 = f32[16,384,64]{1,2,0:T(8,128)} fusion(bf16[1,64,18,386]{3,1,2,0:T(8,128)(2,1)S(1)} %get-tuple-element.6, bf16[3,3,64,64]{3,2,1,0:T(8,128)(2,1)S(1)} %copy-done.2), kind=kOutput, calls=%fused_computation.88 | convolution fusion | flops 50331648 | bytes 2375680 | tf_op jit(solution)/shard_map/oc,boij->bcij/dot_general | solution.py:209
  47.5 1.6 %fusion.34 = f32[16,384,64]{1,2,0:T(8,128)} fusion(bf16[1,64,18,386]{3,1,2,0:T(8,128)(2,1)S(1)} %get-tuple-element.6, bf16[3,3,64,64]{3,2,1,0:T(8,128)(2,1)S(1)} %copy-done.2), kind=kOutput, calls=%fused_computation.90 | convolution fusion | flops 50331648 | bytes 2375680 | tf_op jit(solution)/shard_map/oc,boij->bcij/dot_general | solution.py:209
  49.1 1.7 %fusion.35 = f32[16,384,64]{1,2,0:T(8,128)} fusion(bf16[1,64,18,386]{3,1,2,0:T(8,128)(2,1)S(1)} %get-tuple-element.6, bf16[3,3,64,64]{3,2,1,0:T(8,128)(2,1)S(1)} %copy-done.2), kind=kOutput, calls=%fused_computation.92 | convolution fusion | flops 50331648 | bytes 2375680 | tf_op jit(solution)/shard_map/oc,boij->bcij/dot_general | solution.py:209
  50.8 0.5 convolution_bitcast_fusion.10
  51.3 0.5 convolution_bitcast_fusion.16
  51.9 0.5 convolution_bitcast_fusion.1
  52.3 0.5 convolution_bitcast_fusion.7
  52.9 0.9 pad_maximum_fusion.5
  53.7 1.9 %reshape.237.x_ref = f32[576,128]{1,0:T(8,128)} reshape(f32[2,3,3,64,64]{4,3,2,1,0:T(8,128)} %pad_maximum_fusion.5) | data formatting | bytes 589824 | tf_op jit(solution)/shard_map/reshape | solution.py:265
  55.7 29.4 %shard_map.76 = f32[576,128]{1,0:T(8,128)} custom-call(f32[576,128]{1,0:T(8,128)} %reshape.237.x_ref), custom_call_target="tpu_custom_call" | custom-call | tf_op jit(solution)/shard_map/pallas_call | solution.py:142
  85.1 1.0 %convert_element_type.43 = bf16[576,128]{1,0:T(8,128)(2,1)S(1)} convert(f32[576,128]{1,0:T(8,128)} %shard_map.76) | non-fusion elementwise | flops 73728 | bytes 442368 | tf_op jit(solution)/shard_map/convert_element_type | solution.py:266
  86.1 0.7 fusion.158
  86.7 1.7 %squeeze.87 = bf16[3,3,64,64]{3,2,1,0:T(8,128)(2,1)} reshape(bf16[288,128]{1,0:T(8,128)(2,1)} %get-tuple-element.17) | data formatting | bytes 147456 | tf_op jit(solution)/shard_map/squeeze | solution.py:267
  88.4 1.7 %squeeze.88 = bf16[3,3,64,64]{3,2,1,0:T(8,128)(2,1)} reshape(bf16[288,128]{1,0:T(8,128)(2,1)} %get-tuple-element.16) | data formatting | bytes 147456 | tf_op jit(solution)/shard_map/squeeze | solution.py:267
  90.1 5.4 %fusion.8 = bf16[1,64,16,384]{3,1,2,0:T(8,128)(2,1)S(1)} fusion(f32[16,384,64]{1,2,0:T(8,128)} %fusion.29, f32[16,384,64]{1,2,0:T(8,128)} %fusion.30, f32[16,384,64]{1,2,0:T(8,128)} %fusion.31, f32[16,384,64]{1,2,0:T(8,128)S(1)} %fusion.47, f32[16,384,64]{1,2,0:T(8,128)} %fusion.32, f32[16,384,64]{1,2,0:T(8,128)} %fusion.33, f32[16,384,64]{1,2,0:T(8,128)} %fusion.35, ...), kind=kOutput, calls=%fused_computation.16 | convolution fusion | flops 54657024 | bytes 14958592 | tf_op jit(solution)/shard_map/oc,boij->bcij/dot_general | solution.py:209
  95.4 1.3 %copy.38 = bf16[1,64,16,384]{3,2,1,0:T(8,128)(2,1)} copy(bf16[1,64,16,384]{3,1,2,0:T(8,128)(2,1)S(1)} %fusion.8) | data formatting | bytes 1572864
  (44 shorter events, 7.1 us)
Async XLA Ops:
  0.6 5.2 %copy-start.1 = (bf16[1,64,16,384]{3,2,1,0:T(8,128)(2,1)S(1)}, bf16[1,64,16,384]{3,2,1,0:T(8,128)(2,1)}, u32[]{:S(2)}) copy-start(bf16[1,64,16,384]{3,2,1,0:T(8,128)(2,1)} %param.5) | copy-start | bytes 2359300
  0.6 1.5 %copy-start = (bf16[1,64,16,384]{3,2,1,0:T(8,128)(2,1)S(1)}, bf16[1,64,16,384]{3,2,1,0:T(8,128)(2,1)}, u32[]{:S(2)}) copy-start(bf16[1,64,16,384]{3,2,1,0:T(8,128)(2,1)} %param.6) | copy-start | bytes 2359300
  0.6 5.1 %copy-start.2 = (bf16[3,3,64,64]{3,2,1,0:T(8,128)(2,1)S(1)}, bf16[3,3,64,64]{3,2,1,0:T(8,128)(2,1)}, u32[]{:S(2)}) copy-start(bf16[3,3,64,64]{3,2,1,0:T(8,128)(2,1)} %param.7) | copy-start | bytes 221188
  2.4 3.8 %copy-start.3 = (bf16[3,3,64,64]{3,2,1,0:T(8,128)(2,1)S(1)}, bf16[3,3,64,64]{3,2,1,0:T(8,128)(2,1)}, u32[]{:S(2)}) copy-start(bf16[3,3,64,64]{3,2,1,0:T(8,128)(2,1)} %param.8) | copy-start | bytes 221188
  2.4 4.7 %collective-permute-start = (bf16[2,64,1,384]{3,1,2,0:T(8,128)(2,1)S(1)}, bf16[2,64,1,384]{3,1,2,0:T(8,128)(2,1)S(1)}, u32[]{:S(2)}, u32[]{:S(2)}) collective-permute-start(bf16[2,64,1,384]{3,1,2,0:T(8,128)(2,1)S(1)} %get-tuple-element.10), channel_id=1, source_target_pairs={{0,1},{1,2},{2,3},{3,4},{4,5},{5,6},{6,7},{7,8},{8,9},{9,10},{10,1... | collective-permute-start | bytes 294920 | tf_op jit(solution)/shard_map/ppermute | solution.py:161
  5.5 4.0 %collective-permute-start.1 = (bf16[2,64,1,384]{3,1,2,0:T(8,128)(2,1)S(1)}, bf16[2,64,1,384]{3,1,2,0:T(8,128)(2,1)S(1)}, u32[]{:S(2)}, u32[]{:S(2)}) collective-permute-start(bf16[2,64,1,384]{3,1,2,0:T(8,128)(2,1)S(1)} %get-tuple-element.11), channel_id=1, source_target_pairs={{1,0},{2,1},{3,2},{4,3},{5,4},{6,5},{7,6},{8,7},{9,8},{10,9},{11,1... | collective-permute-start | bytes 294920 | tf_op jit(solution)/shard_map/ppermute | solution.py:162
  6.2 0.7 copy-start.4
  21.4 10.5 %collective-permute-start.2 = (bf16[1,64,1,384]{3,1,2,0:T(8,128)(2,1)S(1)}, bf16[1,64,1,384]{3,1,2,0:T(8,128)(2,1)S(1)}, u32[]{:S(2)}, u32[]{:S(2)}) collective-permute-start(bf16[1,64,1,384]{3,1,2,0:T(8,128)(2,1)S(1)} %get-tuple-element.14), channel_id=1, source_target_pairs={{0,1},{1,2},{2,3},{3,4},{4,5},{5,6},{6,7},{7,8},{8,9},{9,10},{10,1... | collective-permute-start | bytes 147464 | tf_op jit(solution)/shard_map/ppermute | solution.py:161
  21.7 10.2 %collective-permute-start.3 = (bf16[1,64,1,384]{3,1,2,0:T(8,128)(2,1)S(1)}, bf16[1,64,1,384]{3,1,2,0:T(8,128)(2,1)S(1)}, u32[]{:S(2)}, u32[]{:S(2)}) collective-permute-start(bf16[1,64,1,384]{3,1,2,0:T(8,128)(2,1)S(1)} %get-tuple-element.15), channel_id=1, source_target_pairs={{1,0},{2,1},{3,2},{4,3},{5,4},{6,5},{7,6},{8,7},{9,8},{10,9},{11,1... | collective-permute-start | bytes 147464 | tf_op jit(solution)/shard_map/ppermute | solution.py:162
  26.5 9.1 %collective-permute-start.4 = (bf16[1,64,1,384]{3,1,2,0:T(8,128)(2,1)S(1)}, bf16[1,64,1,384]{3,1,2,0:T(8,128)(2,1)S(1)}, u32[]{:S(2)}, u32[]{:S(2)}) collective-permute-start(bf16[1,64,1,384]{3,1,2,0:T(8,128)(2,1)S(1)} %get-tuple-element.12), channel_id=1, source_target_pairs={{0,1},{1,2},{2,3},{3,4},{4,5},{5,6},{6,7},{7,8},{8,9},{9,10},{10,1... | collective-permute-start | bytes 147464 | tf_op jit(solution)/shard_map/ppermute | solution.py:161
  26.5 9.1 %collective-permute-start.5 = (bf16[1,64,1,384]{3,1,2,0:T(8,128)(2,1)S(1)}, bf16[1,64,1,384]{3,1,2,0:T(8,128)(2,1)S(1)}, u32[]{:S(2)}, u32[]{:S(2)}) collective-permute-start(bf16[1,64,1,384]{3,1,2,0:T(8,128)(2,1)S(1)} %get-tuple-element.13), channel_id=1, source_target_pairs={{1,0},{2,1},{3,2},{4,3},{5,4},{6,5},{7,6},{8,7},{9,8},{10,9},{11,1... | collective-permute-start | bytes 147464 | tf_op jit(solution)/shard_map/ppermute | solution.py:162

commit v2 on v0

v2 whole, which is shorter than its diff:
```python
import functools
import jax
import jax.numpy as jnp
from jax import lax
from jax.experimental import pallas as pl
from jax.experimental.pallas import tpu as pltpu
from jax.sharding import PartitionSpec as P

MESH = pl.DeviceIdType.MESH
TOTAL_ROWS = 576


class Grid:
    def __init__(self, dp_size, lon_size):
        self.high = 2 if lon_size == 32 else 1
        self.deep = lon_size // (2 * self.high)
        self.plane = dp_size * self.high * 2
        self.rows = TOTAL_ROWS // self.plane

    def place(self):
        dp = lax.axis_index("dp")
        lon = lax.axis_index("lon")
        core = lon % 2
        z = (lon // 2) % self.deep
        high = lon // (2 * self.deep)
        return dp, lon, z, (dp * self.high + high) * 2 + core

    def device(self, member, z):
        high = (member // 2) % self.high
        return (member // (2 * self.high), (high * self.deep + z) * 2 + member % 2)

    def greeted(self):
        return self.plane + self.deep - 2

    def greet(self):
        dp, lon, z, member = self.place()
        barrier = pltpu.get_barrier_semaphore()

        def signal(device):
            pl.semaphore_signal(barrier, inc=1, device_id=device, device_id_type=MESH)

        loop(1, self.plane, lambda k: signal(self.device((member + k) % self.plane, z)))
        loop(1, self.deep, lambda k: signal(self.device(member, (z + k) % self.deep)))
        return barrier


class Reduction:
    def __init__(self, grid, flat, factor, out, parts, zparts, whole, plane_send, plane_recv, deep_send, deep_recv, gather_send, gather_recv):
        self.grid, self.flat, self.factor = grid, flat, factor
        self.out, self.parts, self.zparts, self.whole = out, parts, zparts, whole
        self.plane_send, self.plane_recv = plane_send, plane_recv
        self.deep_send, self.deep_recv = deep_send, deep_recv
        self.gather_send, self.gather_recv = gather_send, gather_recv
        self.dp, self.lon, self.z, self.member = grid.place()

    def scatter(self, k, slot):
        peer = (self.member + k) % self.grid.plane
        slot = self.member if slot is None else peer
        return pltpu.make_async_remote_copy(
            src_ref=self.out.at[peer], dst_ref=self.parts.at[slot], send_sem=self.plane_send.at[peer],
            recv_sem=self.plane_recv.at[slot], device_id=self.grid.device(peer, self.z), device_id_type=MESH)

    def across(self, k, slot):
        peer = (self.z + k) % self.grid.deep
        slot = self.z if slot is None else peer
        return pltpu.make_async_remote_copy(
            src_ref=self.zparts.at[self.z], dst_ref=self.zparts.at[slot], send_sem=self.deep_send.at[peer],
            recv_sem=self.deep_recv.at[slot], device_id=self.grid.device(self.member, peer), device_id_type=MESH)

    def gather(self, k, slot):
        peer = (self.member + k) % self.grid.plane
        slot = self.member if slot is None else peer
        return pltpu.make_async_remote_copy(
            src_ref=self.whole.at[self.member], dst_ref=self.whole.at[slot], send_sem=self.gather_send.at[peer],
            recv_sem=self.gather_recv.at[slot], device_id=self.grid.device(peer, self.z), device_id_type=MESH)

    def scatter_start(self):
        rows = self.grid.rows
        for g in range(self.grid.plane):
            self.out[g] = self.flat[g * rows:(g + 1) * rows, :].astype(self.out.dtype)
        self.parts[self.member] = self.out[self.member]
        loop(1, self.grid.plane, lambda k: self.scatter(k, None).start())

    def finish(self):
        plane, deep, rows = self.grid.plane, self.grid.deep, self.grid.rows
        loop(1, plane, lambda k: self.scatter(k, 0).wait_recv())
        total = self.parts[0].astype(F32)
        for g in range(1, plane):
            total = total + self.parts[g].astype(F32)
        self.zparts[self.z] = total.astype(self.zparts.dtype)
        loop(1, deep, lambda k: self.across(k, None).start())
        loop(1, deep, lambda k: self.across(k, 0).wait_recv())
        total = self.zparts[0].astype(F32)
        for g in range(1, deep):
            total = total + self.zparts[g].astype(F32)
        self.whole[self.member] = (total * self.factor).astype(self.whole.dtype)
        loop(1, plane, lambda k: self.gather(k, None).start())
        loop(1, plane, lambda k: self.gather(k, 0).wait_recv())
        for g in range(plane):
            self.flat[g * rows:(g + 1) * rows, :] = self.whole[g].astype(F32)
        loop(1, plane, lambda k: self.scatter(k, None).wait_send())
        loop(1, deep, lambda k: self.across(k, None).wait_send())
        loop(1, plane, lambda k: self.gather(k, None).wait_send())


def net_scratch(grid):
    return [
        pltpu.VMEM((grid.plane, grid.rows, 128), BF16),
        pltpu.VMEM((grid.plane, grid.rows, 128), BF16),
        pltpu.VMEM((grid.deep, grid.rows, 128), F32),
        pltpu.VMEM((grid.plane, grid.rows, 128), BF16),
        pltpu.SemaphoreType.DMA((grid.plane,)),
        pltpu.SemaphoreType.DMA((grid.plane,)),
        pltpu.SemaphoreType.DMA((grid.deep,)),
        pltpu.SemaphoreType.DMA((grid.deep,)),
        pltpu.SemaphoreType.DMA((grid.plane,)),
        pltpu.SemaphoreType.DMA((grid.plane,)),
    ]


C = 64
COLS = 16
LAT = 384
SLOTS = COLS + 4
gelu_coef = 0.7978845608
F32 = jnp.float32
BF16 = jnp.bfloat16
NT = (((1,), (1,)), ((), ()))


def loop(start, stop, fn):
    def step(k, carry):
        fn(k)
        return carry

    lax.fori_loop(start, stop, step, 0)


def moved_rows(x):
    lane = lax.broadcasted_iota(jnp.int32, x.shape, 1)
    zero = jnp.zeros_like(x)
    right = jnp.where(lane == 0, zero, pltpu.roll(x, 1, 1))
    left = jnp.where(lane == LAT - 1, zero, pltpu.roll(x, LAT - 1, 1))
    return jnp.concatenate([right, x, left], axis=0)


def dot(a, b):
    return jnp.dot(a, b, preferred_element_type=F32)


def adjoint_taps(k_ref, p):
    row = lax.broadcasted_iota(jnp.int32, (C, C), 0)
    col = lax.broadcasted_iota(jnp.int32, (C, C), 1)
    one = jnp.where(row == col, 1.0, 0.0).astype(BF16)
    stacked = jnp.concatenate([k_ref[p, 2], k_ref[p, 1], k_ref[p, 0]], axis=0)
    return lax.dot_general(one, stacked, NT, preferred_element_type=F32).astype(BF16)


def step_kernel(grid, factor, f_ref, t_ref, k1_ref, k2_ref, m_ref, out_ref, g1_ref, g2_ref,
                ft, tt, ts, f3, y, z, hid, d, ds, taps, near, far, acc, flat,
                halo_send, halo_recv, *net):
    dp, lon, deep, member = grid.place()
    lon_size = lax.axis_size("lon")
    right = (dp, (lon + 1) % lon_size)
    left = (dp, (lon + lon_size - 1) % lon_size)
    barrier = grid.greet()
    for neighbour in (left, right):
        pl.semaphore_signal(barrier, inc=1, device_id=neighbour, device_id_type=MESH)

    def turn(k):
        rows = pl.ds(pl.multiple_of(k * 16, 16), 16)
        ft[2:2 + COLS, rows, :] = jnp.swapaxes(f_ref[rows], 0, 1)
        tt[2:2 + COLS, rows, :] = jnp.swapaxes(t_ref[rows], 0, 1)

    loop(0, C // 16, turn)
    pl.semaphore_wait(barrier, grid.greeted() + 2)
    copies = []
    for index, ref in enumerate((ft, tt)):
        copies.append(pltpu.make_async_remote_copy(
            src_ref=ref.at[pl.ds(COLS, 2)], dst_ref=ref.at[pl.ds(0, 2)], send_sem=halo_send.at[2 * index],
            recv_sem=halo_recv.at[2 * index], device_id=right, device_id_type=MESH))
        copies.append(pltpu.make_async_remote_copy(
            src_ref=ref.at[pl.ds(2, 2)], dst_ref=ref.at[pl.ds(COLS + 2, 2)], send_sem=halo_send.at[2 * index + 1],
            recv_sem=halo_recv.at[2 * index + 1], device_id=left, device_id_type=MESH))
    for copy in copies:
        copy.start()

    for p in range(3):
        taps[p * C:(p + 1) * C, :] = jnp.concatenate([k1_ref[p, 0], k1_ref[p, 1], k1_ref[p, 2]], axis=1)
    for index, k_ref in enumerate((k1_ref, k2_ref)):
        far[index] = jnp.concatenate([adjoint_taps(k_ref, 0), adjoint_taps(k_ref, 2)], axis=0)
        near[index] = adjoint_taps(k_ref, 1)
    metric = m_ref[...]

    def adjoint_block(index, slot, count, plain, scaled):
        p3 = jnp.concatenate([moved_rows(v) for v in plain], axis=1)
        s3 = jnp.concatenate([moved_rows(v) for v in scaled], axis=1)
        zn = dot(near[index], p3)
        zf = dot(far[index], s3)
        for n in range(count):
            z[slot + n, :2 * C] = zf[:, n * LAT:(n + 1) * LAT]
            z[slot + n, 2 * C:] = zn[:, n * LAT:(n + 1) * LAT]

    def first_block(slot, count):
        rows = []
        plain = []
        scaled = []
        for n in range(count):
            rows.append(moved_rows(ft[slot + n]))
            f3[slot + n] = rows[n]
            plain.append(tt[slot + n])
            scaled.append((plain[n].astype(F32) * metric).astype(BF16))
            ts[slot + n] = scaled[n]
        yb = dot(taps[...], jnp.concatenate(rows, axis=1))
        for n in range(count):
            y[slot + n] = yb[:, n * LAT:(n + 1) * LAT]
        adjoint_block(1, slot, count, plain, scaled)

    loop(0, 4, lambda b: first_block(2 + 4 * b, 4))
    for copy in copies:
        copy.wait_recv()
    loop(0, 2, lambda b: first_block((COLS + 2) * b, 2))

    def adjoint_sum(s):
        return z[s, 2 * C:] + z[s - 1, C:2 * C] + z[s + 1, :C]

    def middle(s):
        u = y[s, C:2 * C] + metric * (y[s - 1, :C] + y[s + 1, 2 * C:])
        square = u * u
        inner = jnp.tanh(gelu_coef * (u + 0.044715 * square * u))
        half = 0.5 * (1.0 + inner)
        slope = half + (0.5 * gelu_coef) * u * (1.0 - inner * inner) * (1.0 + 3.0 * 0.044715 * square)
        hid[s] = (u * half).astype(BF16)
        delta = (adjoint_sum(s) * slope).astype(BF16)
        d[s] = delta
        ds[s] = (delta.astype(F32) * metric).astype(BF16)

    def middle_two(b):
        middle(1 + 2 * b)
        middle(2 + 2 * b)

    loop(0, (COLS + 2) // 2, middle_two)

    acc[...] = jnp.zeros_like(acc)

    def gradient(b):
        s = 2 + 4 * b
        h3 = jnp.concatenate([moved_rows(hid[s + n]) for n in range(4)], axis=1)
        e3 = jnp.concatenate([
            jnp.concatenate([ts[s + n + 1], tt[s + n], ts[s + n - 1]], axis=0) for n in range(4)], axis=1)
        acc[1] += lax.dot_general(e3, h3, NT, preferred_element_type=F32)
        v3 = jnp.concatenate([f3[s + n] for n in range(4)], axis=1)
        d3 = jnp.concatenate([
            jnp.concatenate([ds[s + n + 1], d[s + n], ds[s + n - 1]], axis=0) for n in range(4)], axis=1)
        acc[0] += lax.dot_general(d3, v3, NT, preferred_element_type=F32)

    loop(0, 4, gradient)
    for index in range(2):
        flat[index * 192:(index + 1) * 192, :] = acc[index, :, :128]
        flat[384 + index * 96:384 + (index + 1) * 96, :] = jnp.concatenate(
            [acc[index, :96, 128:], acc[index, 96:, 128:]], axis=1)
    reduction = Reduction(grid, flat, factor, *net)
    reduction.scatter_start()

    def last_block(slot, count):
        adjoint_block(0, slot, count, [d[slot + n] for n in range(count)], [ds[slot + n] for n in range(count)])

    loop(0, 6, lambda b: last_block(1 + 3 * b, 3))

    def finish(s):
        tt[s] = (tt[s].astype(F32) + adjoint_sum(s)).astype(BF16)

    def finish_two(b):
        finish(2 + 2 * b)
        finish(3 + 2 * b)

    for copy in copies:
        copy.wait_send()
    loop(0, COLS // 2, finish_two)

    def turn_back(k):
        rows = pl.ds(pl.multiple_of(k * 16, 16), 16)
        out_ref[rows] = jnp.swapaxes(tt[2:2 + COLS, rows, :], 0, 1)

    loop(0, C // 16, turn_back)
    reduction.finish()
    for index, g_ref in enumerate((g1_ref, g2_ref)):
        for p in range(3):
            base = index * 192 + p * C
            pair = flat[base:base + C, :]
            g_ref[p, 0] = pair[:, :C].astype(BF16)
            g_ref[p, 1] = pair[:, C:].astype(BF16)
        side = flat[384 + index * 96:384 + (index + 1) * 96, :]
        rest = jnp.concatenate([side[:, :C], side[:, C:]], axis=0)
        for p in range(3):
            g_ref[p, 2] = rest[p * C:(p + 1) * C].astype(BF16)


def per_device(fields, cotangent, kernel_first, kernel_second, metric):
    dp_size, lon_size = lax.axis_size("dp"), lax.axis_size("lon")
    grid = Grid(dp_size, lon_size)
    factor = 1.0 / (float(dp_size) * float(COLS * lon_size) * float(LAT)) ** 0.5
    vmem = pl.BlockSpec(memory_space=pltpu.VMEM)
    field_grad, first, second = pl.pallas_call(
        functools.partial(step_kernel, grid, factor),
        out_shape=(
            jax.ShapeDtypeStruct((C, COLS, LAT), BF16),
            jax.ShapeDtypeStruct((3, 3, C, C), BF16),
            jax.ShapeDtypeStruct((3, 3, C, C), BF16),
        ),
        in_specs=[vmem] * 5,
        out_specs=(vmem, vmem, vmem),
        scratch_shapes=[
            pltpu.VMEM((SLOTS, C, LAT), BF16),
            pltpu.VMEM((SLOTS, C, LAT), BF16),
            pltpu.VMEM((SLOTS, C, LAT), BF16),
            pltpu.VMEM((SLOTS, 3 * C, LAT), BF16),
            pltpu.VMEM((SLOTS, 3 * C, LAT), F32),
            pltpu.VMEM((SLOTS, 3 * C, LAT), F32),
            pltpu.VMEM((SLOTS, C, LAT), BF16),
            pltpu.VMEM((SLOTS, C, LAT), BF16),
            pltpu.VMEM((SLOTS, C, LAT), BF16),
            pltpu.VMEM((3 * C, 3 * C), BF16),
            pltpu.VMEM((2, C, 3 * C), BF16),
            pltpu.VMEM((2, 2 * C, 3 * C), BF16),
            pltpu.VMEM((2, 3 * C, 3 * C), F32),
            pltpu.VMEM((TOTAL_ROWS, 128), F32),
            pltpu.SemaphoreType.DMA((4,)),
            pltpu.SemaphoreType.DMA((4,)),
        ] + net_scratch(grid),
        compiler_params=pltpu.CompilerParams(
            collective_id=0, has_side_effects=True, vmem_limit_bytes=56 * 2**20),
    )(fields[0], cotangent[0], kernel_first, kernel_second, metric[None, :])
    return field_grad[None], first, second


def solution(mesh):
    placed = (P("dp", None, "lon", None), P("dp", None, "lon", None), P(), P(), P())
    return jax.shard_map(
        per_device,
        mesh=mesh,
        in_specs=placed,
        out_specs=(P("dp", None, "lon", None), P(), P()),
        check_vma=False,
    )
```

time: 326 us -> 46.8 us (0.14)
  waiting for transfers between devices: 250 us -> 0 us
  Pallas kernels: 0 us -> 41 us
  matrix products: 36 us -> 0 us
  between operations: 14.5 us -> 0.66 us
  starting transfers between devices: 13.7 us -> 0 us
  other arithmetic: 7.25 us -> 0 us
    psum x1 -> x0, waiting for transfers between devices: 248 us -> none  [per_device(): first, second = lax.psum((first, second), ('dp', 'lon'))]
    pallas_call x0 -> x1, Pallas kernels: none -> 41 us  [per_device(): pl.pallas_call(functools.partial(step_kernel, grid, factor), out_shape=(j...]
    dot_general x45 -> x0, matrix products: 36 us -> none  [the longest x18 22.2 us: stencil_adjoint(): jnp.einsum('oc,boij->bcij', taps[p, q], source[:, :, 2 - p:2 - p + column...]
    ppermute x6 -> x0, starting transfers between devices: 13.6 us -> none  [the longest x3 10.4 us: extended(): after = lax.ppermute(first, axis, down)]
    convert_element_type x4 -> x0, other arithmetic: 4.76 us -> none  [the longest x1 1.66 us: per_device(): (second * factor).astype(jnp.bfloat16)]
  transfers between devices with their start and end apart: 7 -> 0, of which waited for: 3 -> 0; matrix products, arithmetic and copies ran while one was open for 3% -> 0% of each run, Pallas kernels for 0% -> 0%
where the time goes in v2:
time: 46.8 us; the launch traced here: 46.6 us
  Pallas kernels  41 us (88%)
  local copies, waits for them, and re-layouts  4.99 us (11%)
  between operations  0.66 us (1%)
    pallas_call x1, Pallas kernels, per_device(): pl.pallas_call(functools.partial(step_kernel, grid, factor), out_shape=(j...  41 us
    unnamed x9, local copies, waits for them, and re-layouts  4.43 us

profile of v2, /device:TPU:1, one launch (start us, length us, event | category | flops | bytes accessed | tf_op | source)
XLA Modules:
  0.0 46.6 jit_solution(15188662558550426643)
XLA Ops:
  0.6 0.0 copy-start.2
  0.6 0.7 %copy-done.2 = f32[384]{0:T(512)S(1)} copy-done((f32[384]{0:T(512)S(1)}, f32[384]{0:T(512)}, u32[]{:S(2)}) %copy-start.2) | copy-done | bytes 1560
  1.3 0.6 %broadcast_in_dim.6.m_ref = f32[1,384]{1,0:T(1,128)} reshape(f32[384]{0:T(512)S(1)} %copy-done.2) | data formatting | bytes 3072 | tf_op jit(solution)/shard_map/broadcast_in_dim | solution.py:333
  1.9 41.0 %shard_map.76 = (bf16[64,16,384]{2,1,0:T(8,128)(2,1)}, bf16[3,3,64,64]{3,2,1,0:T(8,128)(2,1)}, bf16[3,3,64,64]{3,2,1,0:T(8,128)(2,1)}) custom-call(bf16[64,16,384]{2,1,0:T(8,128)(2,1)} %bitcast.4, bf16[64,16,384]{2,1,0:T(8,128)(2,1)} %bitcast.5, bf16[3,3,64,64]{3,2,1,0:T(8,128)(2,1)} %k1_ref.1, bf16[3,3,64,64]{3,2,1,0:T(8,128)(2,1)} %k2_ref.1, ...), custom_call_target="tpu_custom_call" | custom-call | tf_op jit(solution)/shard_map/pallas_call | solution.py:304
  42.9 0.0 copy-start.1
  42.9 2.1 %copy.11 = bf16[1,64,16,384]{3,2,1,0:T(8,128)(2,1)} copy(bf16[1,64,16,384]{3,2,1,0:T(8,128)(2,1)} %bitcast.3) | data formatting | bytes 1572864
  45.0 0.0 copy-done.1
  45.0 0.0 copy-start
  45.0 0.7 %copy.12 = bf16[3,3,64,64]{3,2,1,0:T(8,128)(2,1)} copy(bf16[3,3,64,64]{3,2,1,0:T(8,128)(2,1)S(1)} %copy-done.1) | data formatting | bytes 147456
  45.7 0.3 copy-done
  46.0 0.7 %copy.13 = bf16[3,3,64,64]{3,2,1,0:T(8,128)(2,1)} copy(bf16[3,3,64,64]{3,2,1,0:T(8,128)(2,1)S(1)} %copy-done) | data formatting | bytes 147456
Async XLA Ops:
  0.6 0.7 %copy-start.2 = (f32[384]{0:T(512)S(1)}, f32[384]{0:T(512)}, u32[]{:S(2)}) copy-start(f32[384]{0:T(512)} %param.9) | copy-start | bytes 4612
  42.9 2.1 %copy-start.1 = (bf16[3,3,64,64]{3,2,1,0:T(8,128)(2,1)S(1)}, bf16[3,3,64,64]{3,2,1,0:T(8,128)(2,1)}, u32[]{:S(2)}) copy-start(bf16[3,3,64,64]{3,2,1,0:T(8,128)(2,1)} %get-tuple-element.13) | copy-start | bytes 221188
  45.0 1.0 %copy-start = (bf16[3,3,64,64]{3,2,1,0:T(8,128)(2,1)S(1)}, bf16[3,3,64,64]{3,2,1,0:T(8,128)(2,1)}, u32[]{:S(2)}) copy-start(bf16[3,3,64,64]{3,2,1,0:T(8,128)(2,1)} %get-tuple-element.14) | copy-start | bytes 221188

commit v3 on v2

v3 whole, which is shorter than its diff:
```python
import functools
import jax
import jax.numpy as jnp
from jax import lax
from jax.experimental import pallas as pl
from jax.experimental.pallas import tpu as pltpu
from jax.sharding import PartitionSpec as P

MESH = pl.DeviceIdType.MESH
TOTAL_ROWS = 576
GRAD_ROWS = 288
C = 64
COLS = 16
LAT = 384
SLOTS = COLS + 4
gelu_coef = 0.7978845608
F32 = jnp.float32
BF16 = jnp.bfloat16
NT = (((1,), (1,)), ((), ()))


def loop(start, stop, fn):
    def step(k, carry):
        fn(k)
        return carry

    lax.fori_loop(start, stop, step, 0)


class Grid:
    def __init__(self, dp_size, lon_size):
        self.high = 2 if lon_size == 32 else 1
        self.deep = lon_size // (2 * self.high)
        self.wide = dp_size // 2
        self.tall = 2 * self.high
        self.plane = 2 * self.wide * self.tall
        self.rows = TOTAL_ROWS // self.plane

    def place(self):
        dp = lax.axis_index("dp")
        lon = lax.axis_index("lon")
        x = lax.rem(dp, self.wide)
        y = lax.div(lon, 2 * self.deep) * 2 + lax.div(dp, self.wide)
        z = lax.rem(lax.div(lon, 2), self.deep)
        return x, y, z, lax.rem(lon, 2)

    def device(self, x, y, z, core):
        return (lax.rem(y, 2) * self.wide + x, (lax.div(y, 2) * self.deep + z) * 2 + core)

    def member(self, m, z):
        x = lax.rem(lax.div(m, self.tall), self.wide)
        return self.device(x, lax.rem(m, self.tall), z, lax.div(m, self.wide * self.tall))

    def own(self):
        x, y, z, core = self.place()
        return (core * self.wide + x) * self.tall + y, z

    def greet(self, barrier):
        m, z = self.own()

        def signal(device):
            pl.semaphore_signal(barrier, inc=1, device_id=device, device_id_type=MESH)

        loop(1, self.plane, lambda k: signal(self.member(lax.rem(m + k, self.plane), z)))
        loop(1, self.deep, lambda k: signal(self.member(m, lax.rem(z + k, self.deep))))
        return self.plane + self.deep - 2


def send(src, dst, send_sem, recv_sem, device):
    return pltpu.make_async_remote_copy(
        src_ref=src, dst_ref=dst, send_sem=send_sem, recv_sem=recv_sem, device_id=device, device_id_type=MESH)


class Reduction:
    def __init__(self, grid, factor, out, parts, zparts, whole, plane_sem, deep_sem, gather_sem):
        self.grid, self.factor = grid, factor
        self.out, self.parts, self.zparts, self.whole = out, parts, zparts, whole
        self.plane_sem, self.deep_sem, self.gather_sem = plane_sem, deep_sem, gather_sem
        self.m, self.z = grid.own()

    def scatter(self, k, arrival=False):
        peer = lax.rem(self.m + k, self.grid.plane)
        slot = peer if arrival else self.m
        return send(self.out.at[peer], self.parts.at[slot], self.plane_sem.at[0, peer], self.plane_sem.at[1, slot],
                    self.grid.member(peer, self.z))

    def across(self, k, arrival=False):
        peer = lax.rem(self.z + k, self.grid.deep)
        slot = peer if arrival else self.z
        return send(self.zparts.at[self.z], self.zparts.at[slot], self.deep_sem.at[0, peer], self.deep_sem.at[1, slot],
                    self.grid.member(self.m, peer))

    def gather(self, k, arrival=False):
        peer = lax.rem(self.m + k, self.grid.plane)
        slot = peer if arrival else self.m
        return send(self.whole.at[self.m], self.whole.at[slot], self.gather_sem.at[0, peer], self.gather_sem.at[1, slot],
                    self.grid.member(peer, self.z))

    def start(self, flat):
        rows = self.grid.rows
        for g in range(self.grid.plane):
            self.out[g] = flat[g * rows:(g + 1) * rows, :].astype(BF16)
        loop(1, self.grid.plane, lambda k: self.scatter(k).start())
        self.parts[self.m] = self.out[self.m]

    def finish(self):
        plane, deep = self.grid.plane, self.grid.deep
        loop(1, plane, lambda k: self.scatter(k, True).wait_recv())
        total = self.parts[0].astype(F32)
        for g in range(1, plane):
            total = total + self.parts[g].astype(F32)
        self.zparts[self.z] = total
        loop(1, deep, lambda k: self.across(k).start())
        loop(1, deep, lambda k: self.across(k, True).wait_recv())
        total = self.zparts[0]
        for g in range(1, deep):
            total = total + self.zparts[g]
        self.whole[self.m] = (total * self.factor).astype(BF16)
        loop(1, plane, lambda k: self.gather(k).start())
        loop(1, plane, lambda k: self.scatter(k).wait_send())
        loop(1, deep, lambda k: self.across(k).wait_send())
        loop(1, plane, lambda k: self.gather(k, True).wait_recv())
        loop(1, plane, lambda k: self.gather(k).wait_send())


def net_scratch(grid):
    block = (grid.rows, 128)
    return [
        pltpu.VMEM((grid.plane,) + block, BF16),
        pltpu.VMEM((grid.plane,) + block, BF16),
        pltpu.VMEM((grid.deep,) + block, F32),
        pltpu.VMEM((grid.plane,) + block, BF16),
        pltpu.SemaphoreType.DMA((2, grid.plane)),
        pltpu.SemaphoreType.DMA((2, grid.deep)),
        pltpu.SemaphoreType.DMA((2, grid.plane)),
    ]


def moved_rows(x):
    lane = lax.broadcasted_iota(jnp.int32, x.shape, 1)
    zero = jnp.zeros_like(x)
    right = jnp.where(lane == 0, zero, pltpu.roll(x, 1, 1))
    left = jnp.where(lane == LAT - 1, zero, pltpu.roll(x, LAT - 1, 1))
    return jnp.concatenate([right, x, left], axis=0)


def dot(a, b):
    return jnp.dot(a, b, preferred_element_type=F32)


def adjoint_taps(k_ref, p):
    row = lax.broadcasted_iota(jnp.int32, (C, C), 0)
    col = lax.broadcasted_iota(jnp.int32, (C, C), 1)
    one = jnp.where(row == col, 1.0, 0.0).astype(BF16)
    stacked = jnp.concatenate([k_ref[p, 2], k_ref[p, 1], k_ref[p, 0]], axis=0)
    return lax.dot_general(one, stacked, NT, preferred_element_type=F32).astype(BF16)


def step_kernel(grid, factor, f_any, t_any, k1_any, k2_any, m_any, out_ref, g_ref,
                f_ref, t_ref, k1_ref, k2_ref, m_ref,
                ft, tt, ts, f3, y, z, hid, d, ds, fg, taps, near, far, acc, flat,
                load_sem, halo_send, halo_recv, *net):
    loads = [pltpu.make_async_copy(source, target, load_sem.at[n]) for n, (source, target) in enumerate(
        ((f_any, f_ref), (t_any, t_ref), (k1_any, k1_ref), (k2_any, k2_ref), (m_any, m_ref)))]
    for load in loads:
        load.start()
    dp, lon = lax.axis_index("dp"), lax.axis_index("lon")
    lon_size = lax.axis_size("lon")
    right = (dp, lax.rem(lon + 1, lon_size))
    left = (dp, lax.rem(lon + lon_size - 1, lon_size))
    barrier = pltpu.get_barrier_semaphore()
    for peer in (left, right):
        pl.semaphore_signal(barrier, inc=1, device_id=peer, device_id_type=MESH)
    greeted = 2 + grid.greet(barrier)

    def turner(source, target):
        def turn(k):
            rows = pl.ds(pl.multiple_of(k * 16, 16), 16)
            target[2:2 + COLS, rows, :] = jnp.swapaxes(source[rows], 0, 1)
        return turn

    loads[0].wait()
    loop(0, C // 16, turner(f_ref, ft))
    loads[1].wait()
    loop(0, C // 16, turner(t_ref, tt))
    pl.semaphore_wait(barrier, greeted)
    copies = []
    for index, ref in enumerate((ft, tt)):
        copies.append(send(ref.at[pl.ds(COLS, 2)], ref.at[pl.ds(0, 2)],
                           halo_send.at[2 * index], halo_recv.at[2 * index], right))
        copies.append(send(ref.at[pl.ds(2, 2)], ref.at[pl.ds(COLS + 2, 2)],
                           halo_send.at[2 * index + 1], halo_recv.at[2 * index + 1], left))
    for copy in copies:
        copy.start()

    for load in loads[2:]:
        load.wait()
    for p in range(3):
        taps[p * C:(p + 1) * C, :] = jnp.concatenate([k1_ref[p, 0], k1_ref[p, 1], k1_ref[p, 2]], axis=1)
    for index, k_ref in enumerate((k1_ref, k2_ref)):
        far[index] = jnp.concatenate([adjoint_taps(k_ref, 0), adjoint_taps(k_ref, 2)], axis=0)
        near[index] = adjoint_taps(k_ref, 1)
    metric = m_ref[...].reshape(1, LAT)

    def adjoint_block(index, slots, plain, scaled):
        p3 = jnp.concatenate([moved_rows(v) for v in plain], axis=1)
        s3 = jnp.concatenate([moved_rows(v) for v in scaled], axis=1)
        zn = dot(near[index], p3)
        zf = dot(far[index], s3)
        for n, s in enumerate(slots):
            z[s, :2 * C] = zf[:, n * LAT:(n + 1) * LAT]
            z[s, 2 * C:] = zn[:, n * LAT:(n + 1) * LAT]

    def first_block(slots):
        rows = [moved_rows(ft[s]) for s in slots]
        plain = [tt[s] for s in slots]
        scaled = [(v.astype(F32) * metric).astype(BF16) for v in plain]
        for n, s in enumerate(slots):
            f3[s] = rows[n]
            ts[s] = scaled[n]
        yb = dot(taps[...], jnp.concatenate(rows, axis=1))
        for n, s in enumerate(slots):
            y[s] = yb[:, n * LAT:(n + 1) * LAT]
        adjoint_block(1, slots, plain, scaled)

    def adjoint_sum(s):
        return z[s, 2 * C:] + z[s - 1, C:2 * C] + z[s + 1, :C]

    def middle(s):
        u = y[s, C:2 * C] + metric * (y[s - 1, :C] + y[s + 1, 2 * C:])
        square = u * u
        inner = jnp.tanh(gelu_coef * (u + 0.044715 * square * u))
        half = 0.5 * (1.0 + inner)
        slope = half + (0.5 * gelu_coef) * u * (1.0 - inner * inner) * (1.0 + 3.0 * 0.044715 * square)
        hid[s] = (u * half).astype(BF16)
        delta = (adjoint_sum(s) * slope).astype(BF16)
        d[s] = delta
        ds[s] = (delta.astype(F32) * metric).astype(BF16)

    def middle_two(s):
        middle(s)
        middle(s + 1)

    def trio(plain, scaled, s):
        return jnp.concatenate([scaled[s + 1], plain[s], scaled[s - 1]], axis=0)

    def second_term(slots):
        h3 = jnp.concatenate([moved_rows(hid[s]) for s in slots], axis=1)
        e3 = jnp.concatenate([trio(tt, ts, s) for s in slots], axis=1)
        acc[1] += lax.dot_general(e3, h3, NT, preferred_element_type=F32)

    def first_term(slots):
        v3 = jnp.concatenate([f3[s] for s in slots], axis=1)
        d3 = jnp.concatenate([trio(d, ds, s) for s in slots], axis=1)
        acc[0] += lax.dot_general(d3, v3, NT, preferred_element_type=F32)

    def terms(b):
        second_term([3 + 7 * b + n for n in range(7)])
        first_term([4 + 6 * b + n for n in range(6)])

    acc[...] = jnp.zeros_like(acc)
    loop(0, 4, lambda b: first_block([2 + 4 * b + n for n in range(4)]))
    loop(0, 7, lambda b: middle_two(3 + 2 * b))
    loop(0, 2, terms)
    for copy in copies:
        copy.wait_recv()
    first_block([0, 1, COLS + 2, COLS + 3])
    middle_two(1)
    middle_two(COLS + 1)
    second_term([2, COLS + 1])
    first_term([2, 3, COLS, COLS + 1])

    reduction = Reduction(grid, factor, *net)
    for index in range(2):
        flat[index * GRAD_ROWS:index * GRAD_ROWS + 192, :] = acc[index, :, :128]
        flat[index * GRAD_ROWS + 192:(index + 1) * GRAD_ROWS, :] = jnp.concatenate(
            [acc[index, :96, 128:], acc[index, 96:, 128:]], axis=1)
    reduction.start(flat)

    def last_block(b):
        slots = [1 + 3 * b + n for n in range(3)]
        adjoint_block(0, slots, [d[s] for s in slots], [ds[s] for s in slots])

    def finish(s):
        fg[s - 2] = (tt[s].astype(F32) + adjoint_sum(s)).astype(BF16)

    def finish_two(b):
        finish(2 + 2 * b)
        finish(3 + 2 * b)

    def turn_back(k):
        part = pl.ds(pl.multiple_of(k * 16, 16), 16)
        out_ref[part] = jnp.swapaxes(fg[:, part, :], 0, 1)

    loop(0, 6, last_block)
    loop(0, COLS // 2, finish_two)
    loop(0, C // 16, turn_back)
    for copy in copies:
        copy.wait_send()
    reduction.finish()
    g_ref[...] = reduction.whole[...]


def format_kernel(grid, x_ref, g_ref, out_ref, g1_ref, g2_ref, flat, sem):
    copy = pltpu.make_async_copy(x_ref, out_ref, sem)
    copy.start()
    rows = grid.rows
    for g in range(TOTAL_ROWS // rows):
        flat[g * rows:(g + 1) * rows, :] = g_ref[g].astype(F32)
    for index, ref in enumerate((g1_ref, g2_ref)):
        for p in range(3):
            base = index * GRAD_ROWS + p * C
            pair = flat[base:base + C, :]
            ref[p, 0] = pair[:, :C].astype(BF16)
            ref[p, 1] = pair[:, C:].astype(BF16)
        side = flat[index * GRAD_ROWS + 192:(index + 1) * GRAD_ROWS, :]
        rest = jnp.concatenate([side[:, :C], side[:, C:]], axis=0)
        for p in range(3):
            ref[p, 2] = rest[p * C:(p + 1) * C].astype(BF16)
    copy.wait()


def per_device(fields, cotangent, kernel_first, kernel_second, metric):
    dp_size, lon_size = lax.axis_size("dp"), lax.axis_size("lon")
    grid = Grid(dp_size, lon_size)
    factor = 1.0 / (float(dp_size) * float(COLS * lon_size) * float(LAT)) ** 0.5
    vmem = pl.BlockSpec(memory_space=pltpu.VMEM)
    anywhere = pl.BlockSpec(memory_space=pl.ANY)
    taps = (3, 3, C, C)
    column = pltpu.VMEM((SLOTS, C, LAT), BF16)
    turned, packed = pl.pallas_call(
        functools.partial(step_kernel, grid, factor),
        out_shape=(
            pltpu.VMEM((C, COLS, LAT), BF16),
            pltpu.VMEM((grid.plane, grid.rows, 128), BF16),
        ),
        in_specs=[anywhere] * 5,
        out_specs=(vmem, vmem),
        scratch_shapes=[
            pltpu.VMEM((C, COLS, LAT), BF16),
            pltpu.VMEM((C, COLS, LAT), BF16),
            pltpu.VMEM(taps, BF16),
            pltpu.VMEM(taps, BF16),
            pltpu.VMEM((LAT,), F32),
            column,
            column,
            column,
            pltpu.VMEM((SLOTS, 3 * C, LAT), BF16),
            pltpu.VMEM((SLOTS, 3 * C, LAT), F32),
            pltpu.VMEM((SLOTS, 3 * C, LAT), F32),
            column,
            column,
            column,
            pltpu.VMEM((COLS, C, LAT), BF16),
            pltpu.VMEM((3 * C, 3 * C), BF16),
            pltpu.VMEM((2, C, 3 * C), BF16),
            pltpu.VMEM((2, 2 * C, 3 * C), BF16),
            pltpu.VMEM((2, 3 * C, 3 * C), F32),
            pltpu.VMEM((TOTAL_ROWS, 128), F32),
            pltpu.SemaphoreType.DMA((5,)),
            pltpu.SemaphoreType.DMA((4,)),
            pltpu.SemaphoreType.DMA((4,)),
        ] + net_scratch(grid),
        compiler_params=pltpu.CompilerParams(
            collective_id=0, has_side_effects=True, vmem_limit_bytes=60 * 2**20),
    )(fields[0], cotangent[0], kernel_first, kernel_second, metric)
    field_grad, first, second = pl.pallas_call(
        functools.partial(format_kernel, grid),
        out_shape=(
            jax.ShapeDtypeStruct((C, COLS, LAT), BF16),
            jax.ShapeDtypeStruct(taps, BF16),
            jax.ShapeDtypeStruct(taps, BF16),
        ),
        in_specs=[vmem, vmem],
        out_specs=(anywhere, vmem, vmem),
        scratch_shapes=[pltpu.VMEM((TOTAL_ROWS, 128), F32), pltpu.SemaphoreType.DMA(())],
        compiler_params=pltpu.CompilerParams(vmem_limit_bytes=16 * 2**20),
    )(turned, packed)
    return field_grad[None], first, second


def solution(mesh):
    placed = (P("dp", None, "lon", None), P("dp", None, "lon", None), P(), P(), P())
    return jax.shard_map(
        per_device,
        mesh=mesh,
        in_specs=placed,
        out_specs=(P("dp", None, "lon", None), P(), P()),
        check_vma=False,
    )
```

time: 46.8 us -> 38 us (0.81)
  local copies, waits for them, and re-layouts: 4.99 us -> 0 us
  Pallas kernels: 41 us -> 37.2 us
    unnamed x9 -> x0, local copies, waits for them, and re-layouts: 4.43 us -> none
    pallas_call x1 -> x2, Pallas kernels: 41 us -> 37.2 us  [the longest x1 35.6 us: per_device(): pl.pallas_call(functools.partial(step_kernel, grid, factor), out_shape=(p...]
    broadcast_in_dim x1 -> x0, local copies, waits for them, and re-layouts: 0.56 us -> none  [per_device(): metric[None, :]]
where the time goes in v3:
time: 38 us; the launch traced here: 37.8 us
  Pallas kernels  37.2 us (98%)
  between operations  0.64 us (2%)
    pallas_call x1, Pallas kernels, per_device(): pl.pallas_call(functools.partial(step_kernel, grid, factor), out_shape=(p...  35.6 us
    pallas_call x1, Pallas kernels, per_device(): pl.pallas_call(functools.partial(format_kernel, grid), out_shape=(jax.Sha...  1.64 us

profile of v3, /device:TPU:1, one launch (start us, length us, event | category | flops | bytes accessed | tf_op | source)
XLA Modules:
  0.0 37.8 jit_solution(14892369447480874786)
XLA Ops:
  0.6 35.6 %shard_map.76 = (bf16[64,16,384]{2,1,0:T(8,128)(2,1)S(1)}, bf16[32,18,128]{2,1,0:T(8,128)(2,1)S(1)}) custom-call(bf16[64,16,384]{2,1,0:T(8,128)(2,1)} %bitcast.3, bf16[64,16,384]{2,1,0:T(8,128)(2,1)} %bitcast.4, bf16[3,3,64,64]{3,2,1,0:T(8,128)(2,1)} %k1_any.1, bf16[3,3,64,64]{3,2,1,0:T(8,128)(2,1)} %k2_any.1, f32[384]{0:T(512)} %m_any.1), custom_call_target="tpu_custom_call" | custom-call | tf_op jit(solution)/shard_map/pallas_call | solution.py:331
  36.2 1.6 %shard_map.77 = (bf16[64,16,384]{2,1,0:T(8,128)(2,1)}, bf16[3,3,64,64]{3,2,1,0:T(8,128)(2,1)}, bf16[3,3,64,64]{3,2,1,0:T(8,128)(2,1)}) custom-call(bf16[64,16,384]{2,1,0:T(8,128)(2,1)S(1)} %get-tuple-element.8.x_ref, bf16[32,18,128]{2,1,0:T(8,128)(2,1)S(1)} %get-tuple-element.9.g_ref), custom_call_target="tpu_custom_call" | custom-call | tf_op jit(solution)/shard_map/pallas_call | solution.py:367

commit v4 on v3

--- a/solution.py
+++ b/solution.py
@@ -9,6 +9,8 @@
 MESH = pl.DeviceIdType.MESH
 TOTAL_ROWS = 576
 GRAD_ROWS = 288
+ORDER = -1
+DEEP_TYPE = jnp.float32
 C = 64
 COLS = 16
 LAT = 384
@@ -78,49 +80,89 @@
         self.plane_sem, self.deep_sem, self.gather_sem = plane_sem, deep_sem, gather_sem
         self.m, self.z = grid.own()
 
-    def scatter(self, k, arrival=False):
-        peer = lax.rem(self.m + k, self.grid.plane)
-        slot = peer if arrival else self.m
-        return send(self.out.at[peer], self.parts.at[slot], self.plane_sem.at[0, peer], self.plane_sem.at[1, slot],
-                    self.grid.member(peer, self.z))
+    def offsets(self):
+        found = []
+        for core in range(2):
+            for x in range(self.grid.wide):
+                for y in range(self.grid.tall):
+                    far = min(x, self.grid.wide - x) + min(y, self.grid.tall - y)
+                    found.append((far, core, x, y))
+        found = [item[1:] for item in sorted(found, key=lambda item: ORDER * item[0])]
+        return [item for item in found if item != (0, 0, 0)]
+
+    def plane_copies(self, arrival, source, target, sem):
+        grid = self.grid
+        x, y, z, core = grid.place()
+        xs = [lax.rem(x + k, grid.wide) for k in range(grid.wide)]
+        ys = [lax.rem(y + k, grid.tall) for k in range(grid.tall)]
+        cores = [core, 1 - core]
+        dps = [[lax.rem(v, 2) * grid.wide + u for v in ys] for u in xs]
+        lons = [[(lax.div(v, 2) * grid.deep + z) * 2 + c for v in ys] for c in cores]
+        copies = []
+        for c, u, v in self.offsets():
+            peer = (cores[c] * grid.wide + xs[u]) * grid.tall + ys[v]
+            slot = peer if arrival else self.m
+            copies.append(send(source(peer), target(slot), sem.at[0], sem.at[1], (dps[u][v], lons[c][v])))
+        return copies
+
+    def scatter(self, arrival=False):
+        return self.plane_copies(arrival, lambda peer: self.out.at[peer], lambda slot: self.parts.at[slot], self.plane_sem)
+
+    def gather(self, arrival=False):
+        return self.plane_copies(arrival, lambda peer: self.whole.at[self.m], lambda slot: self.whole.at[slot], self.gather_sem)
 
     def across(self, k, arrival=False):
         peer = lax.rem(self.z + k, self.grid.deep)
         slot = peer if arrival else self.z
-        return send(self.zparts.at[self.z], self.zparts.at[slot], self.deep_sem.at[0, peer], self.deep_sem.at[1, slot],
+        return send(self.zparts.at[self.z], self.zparts.at[slot], self.deep_sem.at[0], self.deep_sem.at[1],
                     self.grid.member(self.m, peer))
 
-    def gather(self, k, arrival=False):
-        peer = lax.rem(self.m + k, self.grid.plane)
-        slot = peer if arrival else self.m
-        return send(self.whole.at[self.m], self.whole.at[slot], self.gather_sem.at[0, peer], self.gather_sem.at[1, slot],
-                    self.grid.member(peer, self.z))
-
-    def start(self, flat):
-        rows = self.grid.rows
-        for g in range(self.grid.plane):
+    def every(self, buffer, sem):
+        block = buffer.at[pl.ds(0, self.grid.plane - 1)]
+        x, y, z, core = self.grid.place()
+        return send(block, block, sem.at[0], sem.at[1], self.grid.device(x, y, z, 1 - core))
+
+    def every_deep(self):
+        block = self.zparts.at[pl.ds(0, self.grid.deep - 1)]
+        x, y, z, core = self.grid.place()
+        return send(block, block, self.deep_sem.at[0], self.deep_sem.at[1], self.grid.device(x, y, z, 1 - core))
+
+    def pack(self, flat, index):
+        rows, half = self.grid.rows, self.grid.plane // 2
+        for g in range(index * half, (index + 1) * half):
             self.out[g] = flat[g * rows:(g + 1) * rows, :].astype(BF16)
-        loop(1, self.grid.plane, lambda k: self.scatter(k).start())
+
+    def start(self):
+        self.scatters = self.scatter()
+        for copy in self.scatters:
+            copy.start()
         self.parts[self.m] = self.out[self.m]
 
+    def after_plane(self):
+        self.every(self.parts, self.plane_sem).wait_recv()
+        total = self.parts[0].astype(F32)
+        for g in range(1, self.grid.plane):
+            total = total + self.parts[g].astype(F32)
+        self.zparts[self.z] = total.astype(self.zparts.dtype)
+        loop(1, self.grid.deep, lambda k: self.across(k).start())
+
+    def after_deep(self):
+        self.every_deep().wait_recv()
+        total = self.zparts[0].astype(F32)
+        for g in range(1, self.grid.deep):
+            total = total + self.zparts[g].astype(F32)
+        self.whole[self.m] = (total * self.factor).astype(BF16)
+        self.gathers = self.gather()
+        for copy in self.gathers:
+            copy.start()
+
+    def drain(self):
+        self.every(self.out, self.plane_sem).wait_send()
+        self.every_deep().wait_send()
+
     def finish(self):
-        plane, deep = self.grid.plane, self.grid.deep
-        loop(1, plane, lambda k: self.scatter(k, True).wait_recv())
-        total = self.parts[0].astype(F32)
-        for g in range(1, plane):
-            total = total + self.parts[g].astype(F32)
-        self.zparts[self.z] = total
-        loop(1, deep, lambda k: self.across(k).start())
-        loop(1, deep, lambda k: self.across(k, True).wait_recv())
-        total = self.zparts[0]
-        for g in range(1, deep):
-            total = total + self.zparts[g]
-        self.whole[self.m] = (total * self.factor).astype(BF16)
-        loop(1, plane, lambda k: self.gather(k).start())
-        loop(1, plane, lambda k: self.scatter(k).wait_send())
-        loop(1, deep, lambda k: self.across(k).wait_send())
-        loop(1, plane, lambda k: self.gather(k, True).wait_recv())
-        loop(1, plane, lambda k: self.gather(k).wait_send())
+        self.every(self.whole, self.gather_sem).wait_recv()
+        self.every(self.whole, self.gather_sem).wait_send()
 
 
 def net_scratch(grid):
@@ -128,11 +170,11 @@
     return [
         pltpu.VMEM((grid.plane,) + block, BF16),
         pltpu.VMEM((grid.plane,) + block, BF16),
-        pltpu.VMEM((grid.deep,) + block, F32),
+        pltpu.VMEM((grid.deep,) + block, DEEP_TYPE),
         pltpu.VMEM((grid.plane,) + block, BF16),
-        pltpu.SemaphoreType.DMA((2, grid.plane)),
-        pltpu.SemaphoreType.DMA((2, grid.deep)),
-        pltpu.SemaphoreType.DMA((2, grid.plane)),
+        pltpu.SemaphoreType.DMA((2,)),
+        pltpu.SemaphoreType.DMA((2,)),
+        pltpu.SemaphoreType.DMA((2,)),
     ]
 
 
@@ -158,8 +200,8 @@
 
 def step_kernel(grid, factor, f_any, t_any, k1_any, k2_any, m_any, out_ref, g_ref,
                 f_ref, t_ref, k1_ref, k2_ref, m_ref,
-                ft, tt, ts, f3, y, z, hid, d, ds, fg, taps, near, far, acc, flat,
-                load_sem, halo_send, halo_recv, *net):
+                ft, tt, ts, f3, y, z, hid, d, ds, fg, dh, taps, near, far, acc, flat,
+                load_sem, halo_send, halo_recv, outer_sem, *net):
     loads = [pltpu.make_async_copy(source, target, load_sem.at[n]) for n, (source, target) in enumerate(
         ((f_any, f_ref), (t_any, t_ref), (k1_any, k1_ref), (k2_any, k2_ref), (m_any, m_ref)))]
     for load in loads:
@@ -175,21 +217,21 @@
 
     def turner(source, target):
         def turn(k):
-            rows = pl.ds(pl.multiple_of(k * 16, 16), 16)
+            rows = pl.ds(k * 16, 16)
             target[2:2 + COLS, rows, :] = jnp.swapaxes(source[rows], 0, 1)
         return turn
 
-    loads[0].wait()
-    loop(0, C // 16, turner(f_ref, ft))
-    loads[1].wait()
-    loop(0, C // 16, turner(t_ref, tt))
+    copies = []
+    for index, (source, ref) in enumerate(((f_ref, ft), (t_ref, tt))):
+        loads[index].wait()
+        for k in range(C // 16):
+            turner(source, ref)(k)
+        pair = [send(ref.at[COLS + 1], ref.at[1],
+                     halo_send.at[2 * index], halo_recv.at[2 * index], right),
+                send(ref.at[2], ref.at[COLS + 2],
+                     halo_send.at[2 * index + 1], halo_recv.at[2 * index + 1], left)]
+        copies += pair
     pl.semaphore_wait(barrier, greeted)
-    copies = []
-    for index, ref in enumerate((ft, tt)):
-        copies.append(send(ref.at[pl.ds(COLS, 2)], ref.at[pl.ds(0, 2)],
-                           halo_send.at[2 * index], halo_recv.at[2 * index], right))
-        copies.append(send(ref.at[pl.ds(2, 2)], ref.at[pl.ds(COLS + 2, 2)],
-                           halo_send.at[2 * index + 1], halo_recv.at[2 * index + 1], left))
     for copy in copies:
         copy.start()
 
@@ -211,17 +253,24 @@
             z[s, :2 * C] = zf[:, n * LAT:(n + 1) * LAT]
             z[s, 2 * C:] = zn[:, n * LAT:(n + 1) * LAT]
 
-    def first_block(slots):
+    def forward_block(slots):
         rows = [moved_rows(ft[s]) for s in slots]
+        for n, s in enumerate(slots):
+            f3[s] = rows[n]
+        yb = dot(taps[...], jnp.concatenate(rows, axis=1))
+        for n, s in enumerate(slots):
+            y[s] = yb[:, n * LAT:(n + 1) * LAT]
+
+    def reverse_block(slots):
         plain = [tt[s] for s in slots]
         scaled = [(v.astype(F32) * metric).astype(BF16) for v in plain]
         for n, s in enumerate(slots):
-            f3[s] = rows[n]
             ts[s] = scaled[n]
-        yb = dot(taps[...], jnp.concatenate(rows, axis=1))
-        for n, s in enumerate(slots):
-            y[s] = yb[:, n * LAT:(n + 1) * LAT]
         adjoint_block(1, slots, plain, scaled)
+
+    def first_block(slots):
+        forward_block(slots)
+        reverse_block(slots)
 
     def adjoint_sum(s):
         return z[s, 2 * C:] + z[s - 1, C:2 * C] + z[s + 1, :C]
@@ -259,44 +308,77 @@
         first_term([4 + 6 * b + n for n in range(6)])
 
     acc[...] = jnp.zeros_like(acc)
-    loop(0, 4, lambda b: first_block([2 + 4 * b + n for n in range(4)]))
-    loop(0, 7, lambda b: middle_two(3 + 2 * b))
-    loop(0, 2, terms)
-    for copy in copies:
+    for s in (0, 1, COLS + 2, COLS + 3):
+        d[s] = jnp.zeros((C, LAT), BF16)
+        ds[s] = jnp.zeros((C, LAT), BF16)
+    for b in range(2):
+        first_block([2 + 8 * b + n for n in range(8)])
+    for b in range(7):
+        middle(3 + b)
+    second_term([3 + n for n in range(7)])
+    for b in range(7, 14):
+        middle(3 + b)
+    second_term([10 + n for n in range(7)])
+    first_term([4 + n for n in range(6)])
+    first_term([10 + n for n in range(6)])
+    reduction = Reduction(grid, factor, *net)
+
+    def pack(index):
+        base = index * GRAD_ROWS
+        flat[base:base + 192, :] = acc[index, :, :128]
+        flat[base + 192:base + GRAD_ROWS, :] = jnp.concatenate([acc[index, :96, 128:], acc[index, 96:, 128:]], axis=1)
+        reduction.pack(flat, index)
+
+    edges = [1, COLS + 2]
+    for copy in copies[:2]:
         copy.wait_recv()
-    first_block([0, 1, COLS + 2, COLS + 3])
-    middle_two(1)
-    middle_two(COLS + 1)
+    forward_block(edges)
+    for copy in copies[2:]:
+        copy.wait_recv()
+    reverse_block(edges)
+    middle(2)
+    middle(COLS + 1)
     second_term([2, COLS + 1])
-    first_term([2, 3, COLS, COLS + 1])
-
-    reduction = Reduction(grid, factor, *net)
-    for index in range(2):
-        flat[index * GRAD_ROWS:index * GRAD_ROWS + 192, :] = acc[index, :, :128]
-        flat[index * GRAD_ROWS + 192:(index + 1) * GRAD_ROWS, :] = jnp.concatenate(
-            [acc[index, :96, 128:], acc[index, 96:, 128:]], axis=1)
-    reduction.start(flat)
-
-    def last_block(b):
-        slots = [1 + 3 * b + n for n in range(3)]
+    pack(1)
+    first_term([1, 2, 3, COLS, COLS + 1, COLS + 2])
+    pack(0)
+    reduction.start()
+    outer = [send(d.at[COLS + 1], dh.at[0], outer_sem.at[0], outer_sem.at[2], right),
+             send(d.at[2], dh.at[1], outer_sem.at[1], outer_sem.at[3], left)]
+    for copy in outer:
+        copy.start()
+
+    def last_block(slots):
         adjoint_block(0, slots, [d[s] for s in slots], [ds[s] for s in slots])
 
     def finish(s):
         fg[s - 2] = (tt[s].astype(F32) + adjoint_sum(s)).astype(BF16)
 
     def finish_two(b):
-        finish(2 + 2 * b)
         finish(3 + 2 * b)
+        finish(4 + 2 * b)
 
     def turn_back(k):
         part = pl.ds(pl.multiple_of(k * 16, 16), 16)
         out_ref[part] = jnp.swapaxes(fg[:, part, :], 0, 1)
 
-    loop(0, 6, last_block)
-    loop(0, COLS // 2, finish_two)
-    loop(0, C // 16, turn_back)
+    loop(0, 4, lambda b: last_block([2 + 4 * b + n for n in range(4)]))
+    loop(0, COLS // 2 - 1, finish_two)
+    reduction.after_plane()
     for copy in copies:
         copy.wait_send()
+    for n, s in enumerate(edges):
+        outer[n].wait_recv()
+        d[s] = dh[n]
+        ds[s] = (dh[n].astype(F32) * metric).astype(BF16)
+    last_block(edges)
+    finish(2)
+    finish(COLS + 1)
+    loop(0, C // 16, turn_back)
+    reduction.after_deep()
+    for copy in outer:
+        copy.wait_send()
+    reduction.drain()
     reduction.finish()
     g_ref[...] = reduction.whole[...]
 
@@ -352,12 +434,14 @@
             column,
             column,
             pltpu.VMEM((COLS, C, LAT), BF16),
+            pltpu.VMEM((2, C, LAT), BF16),
             pltpu.VMEM((3 * C, 3 * C), BF16),
             pltpu.VMEM((2, C, 3 * C), BF16),
             pltpu.VMEM((2, 2 * C, 3 * C), BF16),
             pltpu.VMEM((2, 3 * C, 3 * C), F32),
             pltpu.VMEM((TOTAL_ROWS, 128), F32),
             pltpu.SemaphoreType.DMA((5,)),
+            pltpu.SemaphoreType.DMA((4,)),
             pltpu.SemaphoreType.DMA((4,)),
             pltpu.SemaphoreType.DMA((4,)),
         ] + net_scratch(grid),

time: 38 us -> 34.6 us (0.911)
  Pallas kernels: 37.2 us -> 33.8 us
    pallas_call x1, Pallas kernels: 35.6 us -> 32.2 us  [per_device(): pl.pallas_call(functools.partial(step_kernel, grid, factor), out_shape=(p...]
where the time goes in v4:
time: 34.6 us; the launch traced here: 34.4 us
  Pallas kernels  33.8 us (98%)
  between operations  0.64 us (2%)
    pallas_call x1, Pallas kernels, per_device(): pl.pallas_call(functools.partial(step_kernel, grid, factor), out_shape=(p...  32.2 us
    pallas_call x1, Pallas kernels, per_device(): pl.pallas_call(functools.partial(format_kernel, grid), out_shape=(jax.Sha...  1.64 us

profile of v4, /device:TPU:1, one launch (start us, length us, event | category | flops | bytes accessed | tf_op | source)
XLA Modules:
  0.0 34.4 jit_solution(1680218926917659769)
XLA Ops:
  0.6 32.2 %shard_map.76 = (bf16[64,16,384]{2,1,0:T(8,128)(2,1)S(1)}, bf16[32,18,128]{2,1,0:T(8,128)(2,1)S(1)}) custom-call(bf16[64,16,384]{2,1,0:T(8,128)(2,1)} %bitcast.3, bf16[64,16,384]{2,1,0:T(8,128)(2,1)} %bitcast.4, bf16[3,3,64,64]{3,2,1,0:T(8,128)(2,1)} %k1_any.1, bf16[3,3,64,64]{3,2,1,0:T(8,128)(2,1)} %k2_any.1, f32[384]{0:T(512)} %m_any.1), custom_call_target="tpu_custom_call" | custom-call | tf_op jit(solution)/shard_map/pallas_call | solution.py:413
  32.8 1.6 %shard_map.77 = (bf16[64,16,384]{2,1,0:T(8,128)(2,1)}, bf16[3,3,64,64]{3,2,1,0:T(8,128)(2,1)}, bf16[3,3,64,64]{3,2,1,0:T(8,128)(2,1)}) custom-call(bf16[64,16,384]{2,1,0:T(8,128)(2,1)S(1)} %get-tuple-element.8.x_ref, bf16[32,18,128]{2,1,0:T(8,128)(2,1)S(1)} %get-tuple-element.9.g_ref), custom_call_target="tpu_custom_call" | custom-call | tf_op jit(solution)/shard_map/pallas_call | solution.py:451

commit v5 on v4

--- a/solution.py
+++ b/solution.py
@@ -57,15 +57,26 @@
         x, y, z, core = self.place()
         return (core * self.wide + x) * self.tall + y, z
 
-    def greet(self, barrier):
-        m, z = self.own()
-
-        def signal(device):
-            pl.semaphore_signal(barrier, inc=1, device_id=device, device_id_type=MESH)
-
-        loop(1, self.plane, lambda k: signal(self.member(lax.rem(m + k, self.plane), z)))
-        loop(1, self.deep, lambda k: signal(self.member(m, lax.rem(z + k, self.deep))))
-        return self.plane + self.deep - 2
+    def greet(self, barrier, left, right):
+        x, y, z, core = self.place()
+        xs = [lax.rem(x + k, self.wide) for k in range(self.wide)]
+        ys = [lax.rem(y + k, self.tall) for k in range(self.tall)]
+        cores = [core, 1 - core]
+        dps = [[lax.rem(v, 2) * self.wide + u for v in ys] for u in xs]
+        bases = [lax.div(v, 2) * self.deep for v in ys]
+        targets = []
+        for c in range(2):
+            for u in range(self.wide):
+                for v in range(self.tall):
+                    far = min(u, self.wide - u) + min(v, self.tall - v)
+                    targets.append((far, (dps[u][v], (bases[v] + z) * 2 + cores[c]), c or u or v))
+        for k in range(1, self.deep):
+            targets.append((min(k, self.deep - k), (dps[0][0], (bases[0] + lax.rem(z + k, self.deep)) * 2 + core), True))
+        targets += [(1.5, left, True), (1.5, right, True)]
+        targets = [item for item in sorted(targets, key=lambda item: -item[0]) if item[2]]
+        for item in targets:
+            pl.semaphore_signal(barrier, inc=1, device_id=item[1], device_id_type=MESH)
+        return len(targets)
 
 
 def send(src, dst, send_sem, recv_sem, device):
@@ -90,23 +101,34 @@
         found = [item[1:] for item in sorted(found, key=lambda item: ORDER * item[0])]
         return [item for item in found if item != (0, 0, 0)]
 
-    def plane_copies(self, arrival, source, target, sem):
+    def plane_copies(self, arrival, source, target, sem, goal=None):
         grid = self.grid
         x, y, z, core = grid.place()
         xs = [lax.rem(x + k, grid.wide) for k in range(grid.wide)]
         ys = [lax.rem(y + k, grid.tall) for k in range(grid.tall)]
-        cores = [core, 1 - core]
+        cores = [core, 1 - core] if goal is None else [goal]
         dps = [[lax.rem(v, 2) * grid.wide + u for v in ys] for u in xs]
         lons = [[(lax.div(v, 2) * grid.deep + z) * 2 + c for v in ys] for c in cores]
         copies = []
         for c, u, v in self.offsets():
+            if goal is not None and (c or not (u or v)):
+                continue
             peer = (cores[c] * grid.wide + xs[u]) * grid.tall + ys[v]
             slot = peer if arrival else self.m
             copies.append(send(source(peer), target(slot), sem.at[0], sem.at[1], (dps[u][v], lons[c][v])))
         return copies
 
-    def scatter(self, arrival=False):
-        return self.plane_copies(arrival, lambda peer: self.out.at[peer], lambda slot: self.parts.at[slot], self.plane_sem)
+    def scatter(self, goal):
+        for copy in self.plane_copies(False, lambda peer: self.out.at[peer], lambda slot: self.parts.at[slot], self.plane_sem, goal):
+            copy.start()
+
+    def scatter_partner(self):
+        x, y, z, core = self.grid.place()
+        half = self.grid.plane // 2
+        peer = self.m + half - 2 * half * core
+        send(self.out.at[peer], self.parts.at[self.m], self.plane_sem.at[0], self.plane_sem.at[1],
+             self.grid.device(x, y, z, 1 - core)).start()
+        self.parts[self.m] = self.out[self.m]
 
     def gather(self, arrival=False):
         return self.plane_copies(arrival, lambda peer: self.whole.at[self.m], lambda slot: self.whole.at[slot], self.gather_sem)
@@ -131,12 +153,6 @@
         rows, half = self.grid.rows, self.grid.plane // 2
         for g in range(index * half, (index + 1) * half):
             self.out[g] = flat[g * rows:(g + 1) * rows, :].astype(BF16)
-
-    def start(self):
-        self.scatters = self.scatter()
-        for copy in self.scatters:
-            copy.start()
-        self.parts[self.m] = self.out[self.m]
 
     def after_plane(self):
         self.every(self.parts, self.plane_sem).wait_recv()
@@ -211,9 +227,7 @@
     right = (dp, lax.rem(lon + 1, lon_size))
     left = (dp, lax.rem(lon + lon_size - 1, lon_size))
     barrier = pltpu.get_barrier_semaphore()
-    for peer in (left, right):
-        pl.semaphore_signal(barrier, inc=1, device_id=peer, device_id_type=MESH)
-    greeted = 2 + grid.greet(barrier)
+    greeted = grid.greet(barrier, left, right)
 
     def turner(source, target):
         def turn(k):
@@ -319,8 +333,6 @@
     for b in range(7, 14):
         middle(3 + b)
     second_term([10 + n for n in range(7)])
-    first_term([4 + n for n in range(6)])
-    first_term([10 + n for n in range(6)])
     reduction = Reduction(grid, factor, *net)
 
     def pack(index):
@@ -340,9 +352,12 @@
     middle(COLS + 1)
     second_term([2, COLS + 1])
     pack(1)
-    first_term([1, 2, 3, COLS, COLS + 1, COLS + 2])
+    reduction.scatter(1)
+    first_term([1 + n for n in range(9)])
+    first_term([10 + n for n in range(9)])
     pack(0)
-    reduction.start()
+    reduction.scatter(0)
+    reduction.scatter_partner()
     outer = [send(d.at[COLS + 1], dh.at[0], outer_sem.at[0], outer_sem.at[2], right),
              send(d.at[2], dh.at[1], outer_sem.at[1], outer_sem.at[3], left)]
     for copy in outer:

time: 34.6 us -> 33.5 us (0.968)
  Pallas kernels: 33.8 us -> 32.8 us
    pallas_call x1, Pallas kernels: 32.2 us -> 31.2 us  [per_device(): pl.pallas_call(functools.partial(step_kernel, grid, factor), out_shape=(p...]
where the time goes in v5:
time: 33.5 us; the launch traced here: 33.4 us
  Pallas kernels  32.8 us (98%)
  between operations  0.64 us (2%)
    pallas_call x1, Pallas kernels, per_device(): pl.pallas_call(functools.partial(step_kernel, grid, factor), out_shape=(p...  31.2 us
    pallas_call x1, Pallas kernels, per_device(): pl.pallas_call(functools.partial(format_kernel, grid), out_shape=(jax.Sha...  1.64 us

profile of v5, /device:TPU:1, one launch (start us, length us, event | category | flops | bytes accessed | tf_op | source)
XLA Modules:
  0.0 33.4 jit_solution(17721201531932359171)
XLA Ops:
  0.6 31.2 %shard_map.76 = (bf16[64,16,384]{2,1,0:T(8,128)(2,1)S(1)}, bf16[32,18,128]{2,1,0:T(8,128)(2,1)S(1)}) custom-call(bf16[64,16,384]{2,1,0:T(8,128)(2,1)} %bitcast.3, bf16[64,16,384]{2,1,0:T(8,128)(2,1)} %bitcast.4, bf16[3,3,64,64]{3,2,1,0:T(8,128)(2,1)} %k1_any.1, bf16[3,3,64,64]{3,2,1,0:T(8,128)(2,1)} %k2_any.1, f32[384]{0:T(512)} %m_any.1), custom_call_target="tpu_custom_call" | custom-call | tf_op jit(solution)/shard_map/pallas_call | solution.py:428
  31.8 1.6 %shard_map.77 = (bf16[64,16,384]{2,1,0:T(8,128)(2,1)}, bf16[3,3,64,64]{3,2,1,0:T(8,128)(2,1)}, bf16[3,3,64,64]{3,2,1,0:T(8,128)(2,1)}) custom-call(bf16[64,16,384]{2,1,0:T(8,128)(2,1)S(1)} %get-tuple-element.8.x_ref, bf16[32,18,128]{2,1,0:T(8,128)(2,1)S(1)} %get-tuple-element.9.g_ref), custom_call_target="tpu_custom_call" | custom-call | tf_op jit(solution)/shard_map/pallas_call | solution.py:466

commit v6 on v5

--- a/solution.py
+++ b/solution.py
@@ -160,7 +160,8 @@
         for g in range(1, self.grid.plane):
             total = total + self.parts[g].astype(F32)
         self.zparts[self.z] = total.astype(self.zparts.dtype)
-        loop(1, self.grid.deep, lambda k: self.across(k).start())
+        for k in sorted(range(1, self.grid.deep), key=lambda k: -min(k, self.grid.deep - k)):
+            self.across(k).start()
 
     def after_deep(self):
         self.every_deep().wait_recv()

time: 33.5 us -> 33.2 us (level)
  no operation moved by 1% of the time
where the time goes in v6:
time: 33.2 us; the launch traced here: 33.1 us
  Pallas kernels  32.5 us (98%)
  between operations  0.64 us (2%)
    pallas_call x1, Pallas kernels, per_device(): pl.pallas_call(functools.partial(step_kernel, grid, factor), out_shape=(p...  30.8 us
    pallas_call x1, Pallas kernels, per_device(): pl.pallas_call(functools.partial(format_kernel, grid), out_shape=(jax.Sha...  1.64 us

profile of v6, /device:TPU:1, one launch (start us, length us, event | category | flops | bytes accessed | tf_op | source)
XLA Modules:
  0.0 33.1 jit_solution(15870139446992799291)
XLA Ops:
  0.6 30.8 %shard_map.76 = (bf16[64,16,384]{2,1,0:T(8,128)(2,1)S(1)}, bf16[32,18,128]{2,1,0:T(8,128)(2,1)S(1)}) custom-call(bf16[64,16,384]{2,1,0:T(8,128)(2,1)} %bitcast.3, bf16[64,16,384]{2,1,0:T(8,128)(2,1)} %bitcast.4, bf16[3,3,64,64]{3,2,1,0:T(8,128)(2,1)} %k1_any.1, bf16[3,3,64,64]{3,2,1,0:T(8,128)(2,1)} %k2_any.1, f32[384]{0:T(512)} %m_any.1), custom_call_target="tpu_custom_call" | custom-call | tf_op jit(solution)/shard_map/pallas_call | solution.py:429
  31.5 1.6 %shard_map.77 = (bf16[64,16,384]{2,1,0:T(8,128)(2,1)}, bf16[3,3,64,64]{3,2,1,0:T(8,128)(2,1)}, bf16[3,3,64,64]{3,2,1,0:T(8,128)(2,1)}) custom-call(bf16[64,16,384]{2,1,0:T(8,128)(2,1)S(1)} %get-tuple-element.8.x_ref, bf16[32,18,128]{2,1,0:T(8,128)(2,1)S(1)} %get-tuple-element.9.g_ref), custom_call_target="tpu_custom_call" | custom-call | tf_op jit(solution)/shard_map/pallas_call | solution.py:467
